TPU v7x, 1024 devices: a whole 8x8x8 slice. The times are simulated.
1024 devices in a mesh: mem: 64 (over z, x), lat: 2 (over y_hi), lon: 8 (over y_lo, core).
Axes of the slice: x: 8, y: 8 (y_hi: 2, y_lo: 4; y = y_hi * 4 + y_lo), z: 8, core: 2. Of those that a mesh axis runs over, the one named last changes fastest.
Arguments:
- members: bfloat16 [128, 16, 256, 512], P('mem', None, 'lon', 'lat'), may hold values from -16 to 16
- control_fine: bfloat16 [128, 16, 256, 512], P('mem', None, 'lon', 'lat'), may hold values from -6 to 6
- control_mid: bfloat16 [128, 16, 128, 256], P('mem', None, 'lon', 'lat'), may hold values from -6 to 6
- control_coarse: bfloat16 [128, 16, 64, 128], P('mem', None, 'lon', 'lat'), may hold values from -6 to 6
- vertical: bfloat16 [3, 16, 16], replicated, may hold values from 0 to 0.25
- mid_picks: int32 [384], replicated, may hold values from 0 to 1
- coarse_picks: int32 [192], replicated, may hold values from 0 to 3
- band_radii: int32 [3], replicated, may hold values from 4 to 8
Outputs:
- increment: float32 [8, 512, 512], P('lon', 'mem', 'lat')
Inputs may be any that keep to these rules, and one draw needn't show every extreme that they name: `mid_picks`: entry i of the first 256 entries picks fine row 2 i + entry for middle-band row i; entry j of the rest picks fine column 2 j + entry for middle-band column j. `coarse_picks`: entry i of the first 128 entries picks fine row 4 i + entry for coarse-band row i; entry j of the rest picks fine column 4 j + entry for coarse-band column j. `band_radii`: radius of each band's horizontal taper, in that band's cells.
All inputs are finite; a program needn't handle non-finite values.
Results may differ from a plain program's by a relative error of at most 0.0062.
Values may be sent and summed in bfloat16 or wider, within the bound.
No kernel may reach another device: no remote copies, remote signals or barrier semaphores. Data moves between devices by JAX's collectives and lax.ppermute only.
A program may use at most 32 MiB of HBM per device.

v0:
```python
import math

import jax
import jax.numpy as jnp
from jax import lax
from jax.sharding import PartitionSpec as P

REACH = 8


band_factors = (1, 2, 4)


def extended(cells, sides, width, closed):
    for axis, dim in sides:
        count = lax.axis_size(axis)
        ends = count if closed else count - 1
        head = lax.slice_in_dim(cells, 0, width, axis=dim)
        tail = lax.slice_in_dim(cells, cells.shape[dim] - width, cells.shape[dim], axis=dim)
        cells = jnp.concatenate(
            [
                lax.ppermute(tail, axis, [(i, (i + 1) % count) for i in range(ends)]),
                cells,
                lax.ppermute(head, axis, [((i + 1) % count, i) for i in range(ends)]),
            ],
            axis=dim,
        )
    return cells


def in_blocks(array, dim, devices):
    before, after = (array.shape[:dim], array.shape[dim + 1 :])
    return jnp.moveaxis(array.reshape(*before, devices, -1, *after), dim, 0)


def sent_and_summed(array, axis, dim):
    parts = in_blocks(array, dim, lax.axis_size(axis))
    arrived = lax.all_to_all(parts, axis, split_axis=0, concat_axis=0, tiled=True)
    return arrived.sum(axis=0)


def tap_weights(radius):
    offsets = jnp.arange(-REACH, REACH + 1).astype(jnp.float32)
    reach_now = radius.astype(jnp.float32)
    spread = 0.5 * reach_now
    unnormed = jnp.where(
        jnp.abs(offsets) <= reach_now,
        jnp.exp(-0.5 * jnp.square(offsets / spread)),
        jnp.float32(0.0),
    )
    return (unnormed / jnp.sum(unnormed)).astype(jnp.bfloat16)


def band_matrix(weights, out_length, in_length):
    offset = (
        jnp.arange(in_length, dtype=jnp.int32)[None, :]
        - jnp.arange(out_length, dtype=jnp.int32)[:, None]
        - REACH
    )
    weight_wide = weights.astype(jnp.float32)
    matrix = jnp.zeros((out_length, in_length), jnp.float32)
    for tap_index in range(2 * REACH + 1):
        matrix = matrix + jnp.where(
            offset == tap_index - REACH, weight_wide[tap_index], jnp.float32(0.0)
        )
    return matrix.astype(jnp.bfloat16)


def vertical_mix(vertical_band, control):
    return jnp.einsum(
        "kl,mlcr->mkcr", vertical_band, control, preferred_element_type=jnp.float32
    ).astype(jnp.bfloat16)


def rim_filter(mixed, weights):
    col_count = mixed.shape[2]
    row_count = mixed.shape[3]
    rimmed = extended(mixed, (("lat", 3),), REACH, False)
    row_matrix = band_matrix(weights, row_count, row_count + 2 * REACH)
    across = jnp.einsum(
        "mkcj,ij->mkci", rimmed, row_matrix, preferred_element_type=jnp.float32
    ).astype(jnp.bfloat16)
    wrapped = extended(across, (("lon", 2),), REACH, True)
    col_matrix = band_matrix(weights, col_count, col_count + 2 * REACH)
    return jnp.einsum("cj,mkjr->mkcr", col_matrix, wrapped, preferred_element_type=jnp.float32)


def picker(chosen, factor):
    length = chosen.shape[0]
    target = factor * jnp.arange(length, dtype=jnp.int32)[:, None] + chosen[:, None]
    return (target == jnp.arange(length * factor, dtype=jnp.int32)[None, :]).astype(jnp.bfloat16)


def restrict(members, chosen, factor):
    band_cols = members.shape[2] // factor
    band_rows = members.shape[3] // factor
    row_start = lax.axis_index("lat") * band_rows
    col_start = band_rows * lax.axis_size("lat") + lax.axis_index("lon") * band_cols
    row_pick = picker(lax.dynamic_slice_in_dim(chosen, row_start, band_rows), factor)
    col_pick = picker(lax.dynamic_slice_in_dim(chosen, col_start, band_cols), factor)
    by_rows = jnp.einsum(
        "mkcr,ir->mkci", members, row_pick, preferred_element_type=jnp.float32
    ).astype(jnp.bfloat16)
    return jnp.einsum(
        "jc,mkci->mkji", col_pick, by_rows, preferred_element_type=jnp.float32
    ).astype(jnp.bfloat16)


def on_device(
    members,
    control_fine,
    control_mid,
    control_coarse,
    vertical,
    mid_picks,
    coarse_picks,
    band_radii,
):
    member_total = members.shape[0] * lax.axis_size("mem")
    controls = (control_fine, control_mid, control_coarse)
    chosen_all = (None, mid_picks, coarse_picks)
    filtered_bands = []
    for band_index in range(2):
        weights = tap_weights(band_radii[band_index])
        mixed = vertical_mix(vertical[band_index], controls[band_index])
        filtered_bands.append(rim_filter(mixed, weights))
    coarse_weights = tap_weights(band_radii[2])
    coarse_mixed = vertical_mix(vertical[2], control_coarse)
    filtered_bands.append(rim_filter(coarse_mixed, coarse_weights))
    member_sums = []
    for band_index in range(3):
        factor = band_factors[band_index]
        restricted = members if factor == 1 else restrict(members, chosen_all[band_index], factor)
        product = restricted.astype(jnp.float32) * filtered_bands[band_index]
        member_sums.append(jnp.sum(product, axis=0))
    accumulated = None
    for band_index in range(3):
        factor = band_factors[band_index]
        summed = member_sums[band_index]
        flat = summed.reshape(summed.shape[0] * summed.shape[1], summed.shape[2])
        reduced = sent_and_summed(flat, "mem", 0)
        spread_out = jnp.repeat(jnp.repeat(reduced, factor, axis=0), factor, axis=1)
        accumulated = spread_out if accumulated is None else accumulated + spread_out
    increment = accumulated / math.sqrt(member_total - 1)
    return increment[None, :, :]


def solution(mesh):
    placed = (
        P("mem", None, "lon", "lat"),
        P("mem", None, "lon", "lat"),
        P("mem", None, "lon", "lat"),
        P("mem", None, "lon", "lat"),
        P(),
        P(),
        P(),
        P(),
    )
    return jax.shard_map(
        on_device, mesh=mesh, in_specs=placed, out_specs=P("lon", "mem", "lat"), check_vma=False
    )
```

profile of v0, /device:TPU:113, one launch (start us, length us, event | category | flops | bytes accessed | tf_op | source)
XLA Modules:
  0.0 194.6 jit_solution(7619416522962113511)
XLA Ops:
  0.0 1.0 copy-done
  1.0 1.1 fusion.2
  2.1 0.0 copy-start.2
  2.2 0.0 copy-start.3
  2.2 0.1 fusion.505
  2.3 0.0 copy-start.5
  2.3 0.0 copy-start.1
  2.4 1.4 collective-permute-start
  3.8 7.9 %collective-permute-start.1 = (bf16[2,16,32,8]{3,1,2,0:T(8,128)(2,1)S(1)}, bf16[2,16,32,8]{3,1,2,0:T(8,128)(2,1)S(1)}, u32[]{:S(2)}, u32[]{:S(2)}) collective-permute-start(bf16[2,16,32,8]{3,1,2,0:T(8,128)(2,1)S(1)} %get-tuple-element.8), channel_id=1, source_target_pairs={{8,0},{9,1},{10,2},{11,3},{12,4},{13,5},{14,6},{15,7},{24,16},{25,... | collective-permute-start | bytes 49160 | tf_op jit(solution)/shard_map/ppermute | solution.py:24
  11.7 0.2 fusion.10
  11.9 0.8 fusion.507
  12.7 1.3 collective-permute-start.4
  14.0 0.1 fusion.14
  14.1 0.7 fusion.508
  14.8 1.3 collective-permute-start.8
  16.1 9.1 %collective-permute-start.9 = (bf16[2,16,8,8]{3,1,2,0:T(8,128)(2,1)S(1)}, bf16[2,16,8,8]{3,1,2,0:T(8,128)(2,1)}, u32[]{:S(2)}, u32[]{:S(2)}) collective-permute-start(bf16[2,16,8,8]{3,1,2,0:T(8,128)(2,1)S(1)} %get-tuple-element.14), channel_id=1, source_target_pairs={{8,0},{9,1},{10,2},{11,3},{12,4},{13,5},{14,6},{15,7},{24,16},{25,... | collective-permute-start | bytes 12296 | tf_op jit(solution)/shard_map/ppermute | solution.py:24
  25.2 0.6 fusion.510
  26.5 0.6 fusion.390
  27.2 0.7 convert_convert_fusion.2
  27.8 0.7 fusion.509
  29.1 0.6 fusion.391
  29.7 0.6 convert_convert_fusion.1
  30.3 0.7 fusion.511
  31.0 0.1 dynamic-slice_add_fusion.3
  31.1 0.1 dynamic-slice_add_fusion.2
  31.9 0.7 fusion.392
  32.6 0.7 convert_convert_fusion
  33.3 0.1 dynamic-slice_add_fusion.1
  33.4 0.1 dynamic-slice_add_fusion
  33.4 0.5 fusion.9
  34.0 0.5 fusion.13
  34.5 0.7 fusion.512
  35.2 1.3 collective-permute-start.5
  36.5 11.7 %convolution_convert_fusion.7 = bf16[2,16,8,64]{3,1,2,0:T(8,128)(2,1)S(1)} fusion(bf16[2,16,8,8]{3,1,2,0:T(8,128)(2,1)} %collective-permute-done.9, bf16[2,16,8,64]{3,1,2,0:T(8,128)(2,1)S(1)} %fusion.14, bf16[2,16,8,8]{3,1,2,0:T(8,128)(2,1)} %collective-permute-done.8, f32[]{:T(128)} %bitcast.90, f32[]{:T(128)} %bitcast.89, f32[]{:T(128)} %bitcast.88, ...), kind=kOutput, calls=%fused_computation.24 | convolution fusion | flops 3032064 | bytes 73796 | tf_op jit(solution)/shard_map/mkcj,ij->mkci/dot_general | solution.py:80
  48.2 11.6 %collective-permute-start.10 = (bf16[2,16,8,64]{3,1,2,0:T(8,128)(2,1)S(1)}, bf16[2,16,8,64]{3,1,2,0:T(8,128)(2,1)S(1)}, u32[]{:S(2)}, u32[]{:S(2)}) collective-permute-start(bf16[2,16,8,64]{3,1,2,0:T(8,128)(2,1)S(1)} %convolution_convert_fusion.7), channel_id=1, source_target_pairs={{0,1},{1,2},{2,3},{3,4},{4,5},{5,6},{6,7},{7,0},{8,9},{9,10},{10,1... | collective-permute-start | bytes 98312 | tf_op jit(solution)/shard_map/ppermute | solution.py:22
  59.8 1.9 collective-permute-start.11
  61.8 0.2 pad_maximum_fusion.1
  62.0 11.1 %convolution_convert_fusion.5 = bf16[2,16,16,128]{3,2,1,0:T(8,128)(2,1)S(1)} fusion(bf16[2,16,16,144]{3,1,2,0:T(8,128)(2,1)S(1)} %pad_maximum_fusion.1, f32[]{:T(128)} %bitcast.55, f32[]{:T(128)} %bitcast.54, f32[]{:T(128)} %bitcast.53, f32[]{:T(128)} %bitcast.52, f32[]{:T(128)} %bitcast.51, f32[]{:T(128)} %bitcast.50, f32[]{:T(128)} %bitcast.49, ...), kind=kOutput, calls=%fused_computation.15 | convolution fusion | flops 19916800 | bytes 278596 | tf_op jit(solution)/shard_map/mkcj,ij->mkci/dot_general | solution.py:80
  73.1 5.4 %collective-permute-start.6 = (bf16[2,16,8,128]{3,2,1,0:T(8,128)(2,1)S(1)}, bf16[2,16,8,128]{3,2,1,0:T(8,128)(2,1)S(1)}, u32[]{:S(2)}, u32[]{:S(2)}) collective-permute-start(bf16[2,16,8,128]{3,2,1,0:T(8,128)(2,1)S(1)} %get-tuple-element.9), channel_id=1, source_target_pairs={{0,1},{1,2},{2,3},{3,4},{4,5},{5,6},{6,7},{7,0},{8,9},{9,10},{10,1... | collective-permute-start | bytes 196616 | tf_op jit(solution)/shard_map/ppermute | solution.py:22
  78.6 1.9 collective-permute-start.7
  80.5 0.5 pad_maximum_fusion
  81.0 11.1 %convolution_convert_fusion = bf16[2,16,32,256]{3,2,1,0:T(8,128)(2,1)S(1)} fusion(bf16[2,16,32,272]{3,1,2,0:T(8,128)(2,1)S(1)} %pad_maximum_fusion, f32[]{:T(128)} %bitcast.21, f32[]{:T(128)} %bitcast.20, f32[]{:T(128)} %bitcast.19, f32[]{:T(128)} %bitcast.18, f32[]{:T(128)} %bitcast.17, f32[]{:T(128)} %bitcast.16, f32[]{:T(128)} %bitcast.15, f32[]{:T(128)} %bitcast.14, ...), kind=kOutput, calls=%fused_computation.2 | convolution fusion | flops 146558976 | bytes 1081412 | tf_op jit(solution)/shard_map/mkcj,ij->mkci/dot_general | solution.py:80
  92.1 5.4 %collective-permute-start.2 = (bf16[2,16,8,256]{3,2,1,0:T(8,128)(2,1)S(1)}, bf16[2,16,8,256]{3,2,1,0:T(8,128)(2,1)S(1)}, u32[]{:S(2)}, u32[]{:S(2)}) collective-permute-start(bf16[2,16,8,256]{3,2,1,0:T(8,128)(2,1)S(1)} %get-tuple-element.5), channel_id=1, source_target_pairs={{0,1},{1,2},{2,3},{3,4},{4,5},{5,6},{6,7},{7,0},{8,9},{9,10},{10,1... | collective-permute-start | bytes 393224 | tf_op jit(solution)/shard_map/ppermute | solution.py:22
  97.6 1.9 collective-permute-start.3
  99.6 10.7 %fusion.11 = f32[16,64,8]{1,2,0:T(8,128)S(1)} fusion(f32[2,16,64,8]{2,3,1,0:T(8,128)S(1)} %fusion.13, bf16[2,16,24,64]{3,1,2,0:T(8,128)(2,1)S(1)} %pad_maximum_fusion.2, f32[]{:T(128)} %bitcast.90, f32[]{:T(128)} %bitcast.89, f32[]{:T(128)} %bitcast.88, f32[]{:T(128)} %bitcast.87, f32[]{:T(128)} %bitcast.86, f32[]{:T(128)} %bitcast.85, f32[]{:T(128)} %bitcast.84, ...), kind=kOutput, calls=%fused_computation.20 | convolution fusion | flops 821184 | bytes 196676 | tf_op jit(solution)/shard_map/cj,mkjr->mkcr/dot_general | solution.py:85
  110.3 0.7 reshape.75
  111.0 16.7 %all-to-all-start.2 = ((f32[64,1,128]{2,1,0:T(1,128)}), f32[64,1,128]{2,1,0:T(1,128)S(1)}, u32[]{:S(2)}, u32[]{:S(2)}) async-start(f32[64,1,128]{2,1,0:T(1,128)} %reshape.75), calls=%async_computation.2 | async-start | bytes 65536 | tf_op jit(solution)/shard_map/all_to_all | solution.py:38
  127.7 11.6 %fusion.7 = f32[16,128,16]{1,2,0:T(8,128)} fusion(f32[2,16,128,16]{2,3,1,0:T(8,128)S(1)} %fusion.9, bf16[2,16,8,128]{3,2,1,0:T(8,128)(2,1)S(1)} %collective-permute-done.7, bf16[2,16,16,128]{3,2,1,0:T(8,128)(2,1)S(1)} %convolution_convert_fusion.5, bf16[2,16,8,128]{3,2,1,0:T(8,128)(2,1)S(1)} %collective-permute-done.6, f32[]{:T(128)} %bitcast.55, ...), kind=kOutput, calls=%fused_computation.13 | convolution fusion | flops 5106176 | bytes 655428 | tf_op jit(solution)/shard_map/cj,mkjr->mkcr/dot_general | solution.py:85
  139.3 12.1 %all-to-all-start.1 = ((f32[64,4,128]{2,1,0:T(4,128)}), f32[64,4,128]{2,1,0:T(4,128)S(1)}, u32[]{:S(2)}, u32[]{:S(2)}) async-start(f32[64,4,128]{2,1,0:T(4,128)} %bitcast.61), calls=%async_computation.1 | async-start | bytes 262144 | tf_op jit(solution)/shard_map/all_to_all | solution.py:38
  151.5 11.5 %fusion.1 = f32[16,32,256]{2,1,0:T(8,128)} fusion(bf16[2,16,32,256]{3,2,1,0:T(8,128)(2,1)S(1)} %copy-done.1, bf16[2,16,8,256]{3,2,1,0:T(8,128)(2,1)S(1)} %collective-permute-done.3, bf16[2,16,32,256]{3,2,1,0:T(8,128)(2,1)S(1)} %convolution_convert_fusion, bf16[2,16,8,256]{3,2,1,0:T(8,128)(2,1)S(1)} %collective-permute-done.2, f32[]{:T(128)} %bitcast.21, ...), kind=kOutput, calls=%fused_computation.4 | convolution fusion | flops 28261888 | bytes 1835076 | tf_op jit(solution)/shard_map/cj,mkjr->mkcr/dot_general | solution.py:85
  163.1 0.0 all-to-all-done.1
  163.1 12.1 %all-to-all-start = ((f32[64,8,256]{2,1,0:T(8,128)}), f32[64,8,256]{2,1,0:T(8,128)S(1)}, u32[]{:S(2)}, u32[]{:S(2)}) async-start(f32[64,8,256]{2,1,0:T(8,128)} %bitcast.27), calls=%async_computation | async-start | bytes 1048576 | tf_op jit(solution)/shard_map/all_to_all | solution.py:38
  175.2 0.5 broadcast.160
  175.7 0.7 reduce.2
  176.4 0.1 reshape.76
  176.5 0.1 reduce_sum.98
  176.6 0.1 copy.39
  176.7 0.1 copy.40
  176.8 0.1 reduce_sum.94
  176.9 0.1 copy.35
  177.1 0.1 copy.36
  177.1 16.8 %all-to-all-done = f32[64,8,256]{2,1,0:T(8,128)S(1)} async-done(((f32[64,8,256]{2,1,0:T(8,128)}), f32[64,8,256]{2,1,0:T(8,128)S(1)}, u32[]{:S(2)}, u32[]{:S(2)}) %all-to-all-start) | async-done | bytes 524320 | tf_op jit(solution)/shard_map/all_to_all | solution.py:38
  193.9 0.1 reduce_sum.89
  194.0 0.6 fusion.228
  (31 shorter events, 0.2 us)
Async XLA Ops:
  0.0 1.0 copy-start
  2.1 9.6 %copy-start.2 = (bf16[2,16,16,128]{3,2,1,0:T(8,128)(2,1)S(1)}, bf16[2,16,16,128]{3,2,1,0:T(8,128)(2,1)}, u32[]{:S(2)}) copy-start(bf16[2,16,16,128]{3,2,1,0:T(8,128)(2,1)} %param.10) | copy-start | bytes 393220
  2.1 9.6 %copy-start.4 = (bf16[3,16,16]{2,1,0:T(8,128)(2,1)S(1)}, bf16[3,16,16]{2,1,0:T(8,128)(2,1)}, u32[]{:S(2)}) copy-start(bf16[3,16,16]{2,1,0:T(8,128)(2,1)} %param.12) | copy-start | bytes 4612
  2.2 11.8 %copy-start.3 = (bf16[2,16,8,64]{3,2,1,0:T(8,128)(2,1)S(1)}, bf16[2,16,8,64]{3,2,1,0:T(8,128)(2,1)}, u32[]{:S(2)}) copy-start(bf16[2,16,8,64]{3,2,1,0:T(8,128)(2,1)} %param.11) | copy-start | bytes 98308
  2.3 22.9 %copy-start.5 = (s32[3]{0:T(128)S(1)}, s32[3]{0:T(128)}, u32[]{:S(2)}) copy-start(s32[3]{0:T(128)} %param.15) | copy-start | bytes 40
  2.3 28.7 %copy-start.6 = (s32[384]{0:T(512)S(1)}, s32[384]{0:T(512)}, u32[]{:S(2)}) copy-start(s32[384]{0:T(512)} %param.13) | copy-start | bytes 4612
  2.3 30.9 %copy-start.7 = (s32[192]{0:T(256)S(1)}, s32[192]{0:T(256)}, u32[]{:S(2)}) copy-start(s32[192]{0:T(256)} %param.14) | copy-start | bytes 2308
  2.3 31.1 %copy-start.1 = (bf16[2,16,32,256]{3,2,1,0:T(8,128)(2,1)S(1)}, bf16[2,16,32,256]{3,2,1,0:T(8,128)(2,1)}, u32[]{:S(2)}) copy-start(bf16[2,16,32,256]{3,2,1,0:T(8,128)(2,1)} %param.8) | copy-start | bytes 1572868
  2.4 76.2 %collective-permute-start = (bf16[2,16,32,8]{3,1,2,0:T(8,128)(2,1)S(1)}, bf16[2,16,32,8]{3,1,2,0:T(8,128)(2,1)S(1)}, u32[]{:S(2)}, u32[]{:S(2)}) collective-permute-start(bf16[2,16,32,8]{3,1,2,0:T(8,128)(2,1)S(1)} %get-tuple-element.7), channel_id=1, source_target_pairs={{0,8},{1,9},{2,10},{3,11},{4,12},{5,13},{6,14},{7,15},{16,24},{17,... | collective-permute-start | bytes 49160 | tf_op jit(solution)/shard_map/ppermute | solution.py:22
  3.8 76.7 %collective-permute-start.1 = (bf16[2,16,32,8]{3,1,2,0:T(8,128)(2,1)S(1)}, bf16[2,16,32,8]{3,1,2,0:T(8,128)(2,1)S(1)}, u32[]{:S(2)}, u32[]{:S(2)}) collective-permute-start(bf16[2,16,32,8]{3,1,2,0:T(8,128)(2,1)S(1)} %get-tuple-element.8), channel_id=1, source_target_pairs={{8,0},{9,1},{10,2},{11,3},{12,4},{13,5},{14,6},{15,7},{24,16},{25,... | collective-permute-start | bytes 49160 | tf_op jit(solution)/shard_map/ppermute | solution.py:24
  12.7 47.2 %collective-permute-start.4 = (bf16[2,16,16,8]{3,1,2,0:T(8,128)(2,1)}, bf16[2,16,16,8]{3,1,2,0:T(8,128)(2,1)S(1)}, u32[]{:S(2)}, u32[]{:S(2)}) collective-permute-start(bf16[2,16,16,8]{3,1,2,0:T(8,128)(2,1)} %get-tuple-element.11), channel_id=1, source_target_pairs={{0,8},{1,9},{2,10},{3,11},{4,12},{5,13},{6,14},{7,15},{16,24},{17,... | collective-permute-start | bytes 24584 | tf_op jit(solution)/shard_map/ppermute | solution.py:22
  14.8 20.4 %collective-permute-start.8 = (bf16[2,16,8,8]{3,1,2,0:T(8,128)(2,1)}, bf16[2,16,8,8]{3,1,2,0:T(8,128)(2,1)}, u32[]{:S(2)}, u32[]{:S(2)}) collective-permute-start(bf16[2,16,8,8]{3,1,2,0:T(8,128)(2,1)} %get-tuple-element.13), channel_id=1, source_target_pairs={{0,8},{1,9},{2,10},{3,11},{4,12},{5,13},{6,14},{7,15},{16,24},{17,... | collective-permute-start | bytes 12296 | tf_op jit(solution)/shard_map/ppermute | solution.py:22
  16.1 20.4 %collective-permute-start.9 = (bf16[2,16,8,8]{3,1,2,0:T(8,128)(2,1)S(1)}, bf16[2,16,8,8]{3,1,2,0:T(8,128)(2,1)}, u32[]{:S(2)}, u32[]{:S(2)}) collective-permute-start(bf16[2,16,8,8]{3,1,2,0:T(8,128)(2,1)S(1)} %get-tuple-element.14), channel_id=1, source_target_pairs={{8,0},{9,1},{10,2},{11,3},{12,4},{13,5},{14,6},{15,7},{24,16},{25,... | collective-permute-start | bytes 12296 | tf_op jit(solution)/shard_map/ppermute | solution.py:24
  35.2 26.6 %collective-permute-start.5 = (bf16[2,16,16,8]{3,1,2,0:T(8,128)(2,1)S(1)}, bf16[2,16,16,8]{3,1,2,0:T(8,128)(2,1)S(1)}, u32[]{:S(2)}, u32[]{:S(2)}) collective-permute-start(bf16[2,16,16,8]{3,1,2,0:T(8,128)(2,1)S(1)} %get-tuple-element.12), channel_id=1, source_target_pairs={{8,0},{9,1},{10,2},{11,3},{12,4},{13,5},{14,6},{15,7},{24,16},{25,... | collective-permute-start | bytes 24584 | tf_op jit(solution)/shard_map/ppermute | solution.py:24
  48.2 49.4 %collective-permute-start.10 = (bf16[2,16,8,64]{3,1,2,0:T(8,128)(2,1)S(1)}, bf16[2,16,8,64]{3,1,2,0:T(8,128)(2,1)S(1)}, u32[]{:S(2)}, u32[]{:S(2)}) collective-permute-start(bf16[2,16,8,64]{3,1,2,0:T(8,128)(2,1)S(1)} %convolution_convert_fusion.7), channel_id=1, source_target_pairs={{0,1},{1,2},{2,3},{3,4},{4,5},{5,6},{6,7},{7,0},{8,9},{9,10},{10,1... | collective-permute-start | bytes 98312 | tf_op jit(solution)/shard_map/ppermute | solution.py:22
  59.8 39.7 %collective-permute-start.11 = (bf16[2,16,8,64]{3,1,2,0:T(8,128)(2,1)S(1)}, bf16[2,16,8,64]{3,1,2,0:T(8,128)(2,1)S(1)}, u32[]{:S(2)}, u32[]{:S(2)}) collective-permute-start(bf16[2,16,8,64]{3,1,2,0:T(8,128)(2,1)S(1)} %convolution_convert_fusion.7), channel_id=1, source_target_pairs={{1,0},{2,1},{3,2},{4,3},{5,4},{6,5},{7,6},{0,7},{9,8},{10,9},{11,1... | collective-permute-start | bytes 98312 | tf_op jit(solution)/shard_map/ppermute | solution.py:24
  73.1 54.6 %collective-permute-start.6 = (bf16[2,16,8,128]{3,2,1,0:T(8,128)(2,1)S(1)}, bf16[2,16,8,128]{3,2,1,0:T(8,128)(2,1)S(1)}, u32[]{:S(2)}, u32[]{:S(2)}) collective-permute-start(bf16[2,16,8,128]{3,2,1,0:T(8,128)(2,1)S(1)} %get-tuple-element.9), channel_id=1, source_target_pairs={{0,1},{1,2},{2,3},{3,4},{4,5},{5,6},{6,7},{7,0},{8,9},{9,10},{10,1... | collective-permute-start | bytes 196616 | tf_op jit(solution)/shard_map/ppermute | solution.py:22
  78.6 49.1 %collective-permute-start.7 = (bf16[2,16,8,128]{3,2,1,0:T(8,128)(2,1)S(1)}, bf16[2,16,8,128]{3,2,1,0:T(8,128)(2,1)S(1)}, u32[]{:S(2)}, u32[]{:S(2)}) collective-permute-start(bf16[2,16,8,128]{3,2,1,0:T(8,128)(2,1)S(1)} %get-tuple-element.10), channel_id=1, source_target_pairs={{1,0},{2,1},{3,2},{4,3},{5,4},{6,5},{7,6},{0,7},{9,8},{10,9},{11,1... | collective-permute-start | bytes 196616 | tf_op jit(solution)/shard_map/ppermute | solution.py:24
  92.1 59.4 %collective-permute-start.2 = (bf16[2,16,8,256]{3,2,1,0:T(8,128)(2,1)S(1)}, bf16[2,16,8,256]{3,2,1,0:T(8,128)(2,1)S(1)}, u32[]{:S(2)}, u32[]{:S(2)}) collective-permute-start(bf16[2,16,8,256]{3,2,1,0:T(8,128)(2,1)S(1)} %get-tuple-element.5), channel_id=1, source_target_pairs={{0,1},{1,2},{2,3},{3,4},{4,5},{5,6},{6,7},{7,0},{8,9},{9,10},{10,1... | collective-permute-start | bytes 393224 | tf_op jit(solution)/shard_map/ppermute | solution.py:22
  97.6 53.9 %collective-permute-start.3 = (bf16[2,16,8,256]{3,2,1,0:T(8,128)(2,1)S(1)}, bf16[2,16,8,256]{3,2,1,0:T(8,128)(2,1)S(1)}, u32[]{:S(2)}, u32[]{:S(2)}) collective-permute-start(bf16[2,16,8,256]{3,2,1,0:T(8,128)(2,1)S(1)} %get-tuple-element.6), channel_id=1, source_target_pairs={{1,0},{2,1},{3,2},{4,3},{5,4},{6,5},{7,6},{0,7},{9,8},{10,9},{11,1... | collective-permute-start | bytes 393224 | tf_op jit(solution)/shard_map/ppermute | solution.py:24
  111.0 28.3 %all-to-all-start.2 = ((f32[64,1,128]{2,1,0:T(1,128)}), f32[64,1,128]{2,1,0:T(1,128)S(1)}, u32[]{:S(2)}, u32[]{:S(2)}) async-start(f32[64,1,128]{2,1,0:T(1,128)} %reshape.75), calls=%async_computation.2 | async-start | bytes 65536 | tf_op jit(solution)/shard_map/all_to_all | solution.py:38
  139.3 23.8 %all-to-all-start.1 = ((f32[64,4,128]{2,1,0:T(4,128)}), f32[64,4,128]{2,1,0:T(4,128)S(1)}, u32[]{:S(2)}, u32[]{:S(2)}) async-start(f32[64,4,128]{2,1,0:T(4,128)} %bitcast.61), calls=%async_computation.1 | async-start | bytes 262144 | tf_op jit(solution)/shard_map/all_to_all | solution.py:38
  163.1 30.8 %all-to-all-start = ((f32[64,8,256]{2,1,0:T(8,128)}), f32[64,8,256]{2,1,0:T(8,128)S(1)}, u32[]{:S(2)}, u32[]{:S(2)}) async-start(f32[64,8,256]{2,1,0:T(8,128)} %bitcast.27), calls=%async_computation | async-start | bytes 1048576 | tf_op jit(solution)/shard_map/all_to_all | solution.py:38
where the time goes:
time: 196 us; the launch traced here: 195 us
  starting transfers between devices  91.5 us (47%)
  matrix products  70.2 us (36%)
  waiting for transfers between devices  16.9 us (9%)
  local copies, waits for them, and re-layouts  7.26 us (4%)
  other arithmetic  6.41 us (3%)
  between operations  2.37 us (1%)
    all_to_all x3, starting transfers between devices, sent_and_summed(): lax.all_to_all(parts, axis, split_axis=0, concat_axis=0, tiled=True)  40.9 us
    dot_general x3, matrix products, rim_filter(): jnp.einsum('cj,mkjr->mkcr', col_matrix, wrapped, preferred_element_type=j...  33.9 us
    dot_general x3, matrix products, rim_filter(): jnp.einsum('mkcj,ij->mkci', rimmed, row_matrix, preferred_element_type=jn...  33.9 us
    ppermute x6, starting transfers between devices, extended(): lax.ppermute(tail, axis, [(i, (i + 1) % count) for i in range(ends)])  26.5 us
    ppermute x6, starting transfers between devices, extended(): lax.ppermute(head, axis, [((i + 1) % count, i) for i in range(ends)])  24.1 us
    all_to_all x3, waiting for transfers between devices, sent_and_summed(): lax.all_to_all(parts, axis, split_axis=0, concat_axis=0, tiled=True)  16.8 us
  transfers between devices with their start and end apart: 15, of which 1 were waited for; matrix products, arithmetic and copies ran while one was open for 42% of the time, Pallas kernels for 0%

commit v1 on v0

v1 whole, which is shorter than its diff:
```python
import functools
import math

import jax
import jax.numpy as jnp
from jax import lax
from jax.experimental import pallas as pl
from jax.experimental.pallas import tpu as pltpu
from jax.sharding import PartitionSpec as P

REACH = 8
LEV = 16
FACTORS = (1, 2, 4)
B16 = jnp.bfloat16
F32 = jnp.float32


def iota(shape, dim):
    return lax.broadcasted_iota(jnp.int32, shape, dim)


def dot(a, b, ca=1, cb=0):
    return lax.dot_general(a, b, (((ca,), (cb,)), ((), ())), preferred_element_type=F32)


def bell(offset, radius):
    wide = offset.astype(F32)
    reach_now = jnp.broadcast_to(radius.astype(F32), wide.shape)
    raw = jnp.exp(-0.5 * jnp.square(wide / (0.5 * reach_now)))
    return jnp.where(jnp.abs(wide) <= reach_now, raw, 0.0)


def bell_sum(radius):
    lanes = iota((8, 128), 1)
    raw = jnp.where(lanes <= 2 * REACH, bell(lanes - REACH, radius), 0.0)
    return jnp.sum(raw, axis=1, keepdims=True)[0:1]


def taps(offset, radius, total):
    return (bell(offset, radius) / total).astype(B16)


def edge_kernel(sizes, fine, mid, coarse, out):
    low_half = lax.axis_index("lat") == 0
    start = 0
    for ref, (cells, rows) in zip((fine, mid, coarse), sizes):
        base = jnp.where(low_half, rows - REACH, 0)
        pick = (iota((REACH, rows), 1) == iota((REACH, rows), 0) + base).astype(B16)
        out[:, start : start + cells] = dot(pick, ref[...], 1, 1).astype(B16)
        start += cells


def prep_kernel(
    sizes,
    radii,
    members,
    vertical,
    mid_picks,
    coarse_picks,
    row0,
    row1,
    row2,
    rim,
    own0,
    own1,
    own2,
    side0,
    side1,
    side2,
    res1,
    res2,
    spare,
):
    lat = lax.axis_index("lat")
    lon = lax.axis_index("lon")
    cols = sizes[0][0] // members.shape[0] * 32
    bands = zip(FACTORS, sizes, (row0, row1, row2), (own0, own1, own2), (side0, side1, side2))
    for band, (factor, (cells, rows), row_ref, own_ref, side_ref) in enumerate(bands):
        radius = radii[band]
        total = bell_sum(radius)
        width = cols // factor
        row_ref[...] = taps(iota((rows, rows), 0) - iota((rows, rows), 1), radius, total)
        base = jnp.where(lat == 0, rows, -REACH)
        shape = (REACH, rows)
        rim[band, :, :rows] = taps(iota(shape, 0) + base - iota(shape, 1), radius, total)
        for ref, span in ((own_ref, width), (side_ref, REACH)):
            lanes = LEV * span
            shape = (cols, lanes)
            place = iota(shape, 1) % span
            target = iota(shape, 0) // factor
            level = (iota((LEV, lanes), 0) == iota((LEV, lanes), 1) // span).astype(B16)
            spread = dot(vertical[band], level)
            if span == width and ref is own_ref:
                parts = ((0, taps(place - target, radius, total)),)
            else:
                parts = (
                    (0, taps(place - REACH - target, radius, total)),
                    (lanes, taps(place + width - target, radius, total)),
                )
            for at, pattern in parts:
                pattern = pattern.astype(F32)
                for k in range(LEV):
                    block = (spread[k : k + 1] * pattern).astype(B16)
                    ref[k * cols : (k + 1) * cols, at : at + lanes] = block
    full_rows = sizes[0][1]
    block = 8 * cols
    for factor, picks, out in ((2, mid_picks, res1), (4, coarse_picks, res2)):
        n = picks.shape[1]
        rows = full_rows // factor
        width = cols // factor
        values = jnp.broadcast_to(picks[...].astype(F32), (8, n)).astype(B16)
        shape = (n, full_rows)
        hot = (iota(shape, 0) == lat * rows + iota(shape, 1) // factor).astype(B16)
        chosen = dot(values, hot)[0:1]
        shape = (full_rows, full_rows)
        wanted = (factor * (iota((1, full_rows), 1) // factor)).astype(F32) + chosen
        row_pick = (iota(shape, 0).astype(F32) == wanted).astype(B16)
        shape = (cols, n)
        hot = (iota(shape, 1) == 2 * rows + lon * width + iota(shape, 0) // factor).astype(B16)
        chosen = dot(hot, values, 1, 1)[:, 0:1]
        wanted = (factor * (iota((cols, 1), 0) // factor)).astype(F32) + chosen
        lanes = iota((cols, block), 1).astype(F32)
        for k in range(8):
            spare[k * cols : (k + 1) * cols] = (lanes == wanted + F32(k * cols)).astype(B16)
        col_pick = spare[...]
        for part in range(members.shape[0] // block):
            at = slice(part * block, (part + 1) * block)
            by_rows = dot(members[at], row_pick).astype(B16)
            out[at] = dot(col_pick, by_rows).astype(B16)


def rows_kernel(sizes, fine, mid, coarse, rim_in, row0, row1, row2, rim, out0, out1, out2, right, left):
    start = 0
    lane = 0
    bands = zip(FACTORS, sizes, (fine, mid, coarse), (row0, row1, row2), (out0, out1, out2))
    for band, (factor, (cells, rows), ref, row_ref, out) in enumerate(bands):
        width = 32 // factor
        matrix = row_ref[...]
        edge = rim[band, :, :rows]
        chunk = 128
        groups = chunk // width
        for part in range(cells // chunk):
            at = slice(part * chunk, (part + 1) * chunk)
            arrived = rim_in[:, start + part * chunk : start + (part + 1) * chunk]
            across = dot(ref[at], matrix) + dot(arrived, edge, 0, 0)
            out[at] = across.astype(B16)
            cut = across.reshape(groups, width, rows)
            to = slice(part * groups * REACH, (part + 1) * groups * REACH)
            right[to, lane : lane + rows] = cut[:, width - REACH :].reshape(-1, rows).astype(B16)
            left[to, lane : lane + rows] = cut[:, :REACH].reshape(-1, rows).astype(B16)
        start += cells
        lane += rows


def widen(values, factor):
    if factor == 1:
        return values
    rows = values.shape[1]
    shape = (rows, rows * factor)
    return dot(values, (iota(shape, 0) == iota(shape, 1) // factor).astype(B16)).astype(B16)


def own_kernel(sizes, acr0, acr1, acr2, own0, own1, own2, members, res1, res2, out):
    first = True
    bands = zip(FACTORS, sizes, (acr0, acr1, acr2), (own0, own1, own2), (members, res1, res2))
    for factor, (cells, rows), acr, own, res in bands:
        half = cells // 2
        size = res.shape[0] // 2
        for m in range(2):
            local = dot(own[...], widen(acr[m * half : (m + 1) * half], factor))
            product = local * res[m * size : (m + 1) * size].astype(F32)
            out[...] = product if first else out[...] + product
            first = False


def side_kernel(sizes, from_left, from_right, side0, side1, side2, members, res1, res2, partial, out, total):
    lane = 0
    total[...] = partial[...]
    bands = zip(FACTORS, sizes, (side0, side1, side2), (members, res1, res2))
    for factor, (cells, rows), side, res in bands:
        half = from_left.shape[0] // 2
        size = res.shape[0] // 2
        for m in range(2):
            at = slice(m * half, (m + 1) * half)
            both = jnp.concatenate(
                [from_left[at, lane : lane + rows], from_right[at, lane : lane + rows]], axis=0
            )
            local = dot(side[...], widen(both, factor))
            total[...] += local * res[m * size : (m + 1) * size].astype(F32)
        lane += rows
    out[...] = total[...].astype(B16)


VMEM = pl.BlockSpec(memory_space=pltpu.VMEM)
SMEM = pl.BlockSpec(memory_space=pltpu.SMEM)


def call(kernel, outs, in_specs, scratch=(), flops=0, limit=24):
    shapes = [jax.ShapeDtypeStruct(shape, kind) for shape, kind in outs]
    many = len(shapes) > 1
    return pl.pallas_call(
        kernel,
        out_shape=shapes if many else shapes[0],
        in_specs=in_specs,
        out_specs=[VMEM] * len(shapes) if many else VMEM,
        scratch_shapes=scratch,
        compiler_params=pltpu.CompilerParams(vmem_limit_bytes=limit << 20),
        cost_estimate=pl.CostEstimate(flops=flops, bytes_accessed=1 << 20, transcendentals=0),
    )


def on_device(
    members,
    control_fine,
    control_mid,
    control_coarse,
    vertical,
    mid_picks,
    coarse_picks,
    band_radii,
):
    devices = lax.axis_size("mem")
    member_total = members.shape[0] * devices
    held = members.shape[0] * LEV
    members = members.reshape(held * members.shape[2], members.shape[3])
    controls = [c.reshape(held * c.shape[2], c.shape[3]) for c in (control_fine, control_mid, control_coarse)]
    sizes = tuple(c.shape for c in controls)
    all_cells = sum(cells for cells, _ in sizes)
    all_rows = sum(rows for _, rows in sizes)
    fine_cells, fine_rows = sizes[0]
    out_cells = fine_cells // 2

    edge = call(
        functools.partial(edge_kernel, sizes), [((REACH, all_cells), B16)], [VMEM] * 3, flops=10**7
    )(*controls)
    with jax.named_scope("lat_swap"):
        arrived = lax.ppermute(edge, "lat", [(0, 1), (1, 0)])

    outs = [((rows, rows), B16) for _, rows in sizes]
    outs += [((3, REACH, fine_rows), B16)]
    outs += [((out_cells, cells // 2), B16) for cells, _ in sizes]
    outs += [((out_cells, 2 * LEV * REACH), B16)] * 3
    outs += [((fine_cells, fine_rows), B16)] * 2
    prep = call(
        functools.partial(prep_kernel, sizes),
        outs,
        [SMEM] + [VMEM] * 4,
        [pltpu.VMEM((256, 256), B16)],
        flops=10**9,
    )(band_radii, members, vertical, mid_picks[None], coarse_picks[None])
    rows = prep[0:3]
    rim = prep[3]
    own = prep[4:7]
    side = prep[7:10]
    res = prep[10:12]

    filtered = call(
        functools.partial(rows_kernel, sizes),
        [(s, B16) for s in sizes] + [((held * REACH, all_rows), B16)] * 2,
        [VMEM] * 8,
        flops=2 * 10**8,
    )(*controls, arrived, *rows, rim)
    across = filtered[0:3]
    count = lax.axis_size("lon")
    with jax.named_scope("lon_right"):
        from_left = lax.ppermute(filtered[3], "lon", [(i, (i + 1) % count) for i in range(count)])
    with jax.named_scope("lon_left"):
        from_right = lax.ppermute(filtered[4], "lon", [((i + 1) % count, i) for i in range(count)])

    partial = call(
        functools.partial(own_kernel, sizes),
        [((out_cells, fine_rows), F32)],
        [VMEM] * 9,
        flops=10**9,
    )(*across, *own, members, *res)
    field = call(
        functools.partial(side_kernel, sizes),
        [((out_cells, fine_rows), B16)],
        [VMEM] * 9,
        [pltpu.VMEM((out_cells, fine_rows), F32)],
        flops=10**9,
    )(from_left, from_right, *side, members, *res, partial)

    blocks = field.reshape(devices, out_cells // devices, fine_rows)
    blocks = lax.all_to_all(blocks, "mem", split_axis=0, concat_axis=0, tiled=True)
    increment = blocks.astype(F32).sum(axis=0) / math.sqrt(member_total - 1)
    return increment[None, :, :]


def solution(mesh):
    placed = (
        P("mem", None, "lon", "lat"),
        P("mem", None, "lon", "lat"),
        P("mem", None, "lon", "lat"),
        P("mem", None, "lon", "lat"),
        P(),
        P(),
        P(),
        P(),
    )
    return jax.shard_map(
        on_device, mesh=mesh, in_specs=placed, out_specs=P("lon", "mem", "lat"), check_vma=False
    )
```

time: 196 us -> 66.2 us (0.34)
  the two profiles are of different devices: /device:TPU:113 before, /device:TPU:1 now
where the time goes in v1:
time: 66.2 us; the launch traced here: 65.8 us
  blocking collectives  31.4 us (47%)
  starting transfers between devices  25 us (38%)
  Pallas kernels  5.13 us (8%)
  local copies, waits for them, and re-layouts  3.46 us (5%)
  other arithmetic  0.67 us (1%)
    all_to_all x1, blocking collectives, on_device(): lax.all_to_all(blocks, 'mem', split_axis=0, concat_axis=0, tiled=True)  31.4 us
    ppermute x1, starting transfers between devices, on_device(): lax.ppermute(filtered[4], 'lon', [((i + 1) % count, i) for i in range(cou...  13 us
    ppermute x1, starting transfers between devices, on_device(): arrived = lax.ppermute(edge, 'lat', [(0, 1), (1, 0)])  8.74 us
    unnamed x22, local copies, waits for them, and re-layouts  3.45 us
    ppermute x1, starting transfers between devices, on_device(): lax.ppermute(filtered[3], 'lon', [(i, (i + 1) % count) for i in range(cou...  3.26 us
    pallas_call x1, Pallas kernels, on_device(): call(functools.partial(prep_kernel, sizes), outs, [SMEM] + [VMEM] * 4, [p...  2.19 us
  transfers between devices with their start and end apart: 3, of which 0 were waited for; matrix products, arithmetic and copies ran while one was open for 0% of the time, Pallas kernels for 5%

profile of v1, /device:TPU:1, one launch (start us, length us, event | category | flops | bytes accessed | tf_op | source)
XLA Modules:
  0.0 65.8 jit_solution(6082602741645885950)
XLA Ops:
  0.0 0.0 copy-start
  0.0 1.0 %copy-done = bf16[2,16,32,256]{3,2,1,0:T(8,128)(2,1)S(1)} copy-done((bf16[2,16,32,256]{3,2,1,0:T(8,128)(2,1)S(1)}, bf16[2,16,32,256]{3,2,1,0:T(8,128)(2,1)}, u32[]{:S(2)}) %copy-start) | copy-done | bytes 524312
  1.0 0.0 copy-start.3
  1.0 0.9 %copy-done.3 = bf16[2,16,16,128]{3,2,1,0:T(8,128)(2,1)S(1)} copy-done((bf16[2,16,16,128]{3,2,1,0:T(8,128)(2,1)S(1)}, bf16[2,16,16,128]{3,2,1,0:T(8,128)(2,1)}, u32[]{:S(2)}) %copy-start.3) | copy-done | bytes 131096
  1.9 0.0 copy-start.5
  1.9 0.8 %copy-done.5 = bf16[2,16,8,64]{3,2,1,0:T(8,128)(2,1)S(1)} copy-done((bf16[2,16,8,64]{3,2,1,0:T(8,128)(2,1)S(1)}, bf16[2,16,8,64]{3,2,1,0:T(8,128)(2,1)}, u32[]{:S(2)}) %copy-start.5) | copy-done | bytes 32792
  2.8 0.0 copy-start.10
  2.8 0.0 copy-start.2
  2.8 0.0 copy-start.7
  2.8 0.3 shard_map.82
  3.1 8.7 %collective-permute-start = (bf16[8,1792]{1,0:T(8,128)(2,1)S(1)}, bf16[8,1792]{1,0:T(8,128)(2,1)S(1)}, u32[]{:S(2)}, u32[]{:S(2)}) collective-permute-start(bf16[8,1792]{1,0:T(8,128)(2,1)S(1)} %shard_map.82), channel_id=1, source_target_pairs={{0,8},{8,0},{1,9},{9,1},{2,10},{10,2},{3,11},{11,3},{4,12},{12,4},... | collective-permute-start | bytes 86024 | tf_op jit(solution)/shard_map/lat_swap/ppermute | solution.py:237
  11.8 0.0 copy-done.10
  11.9 0.0 copy-start.8
  11.9 0.0 copy-start.9
  11.9 0.0 copy-done.2
  11.9 0.0 copy-done.7
  11.9 0.6 copy-done.8
  12.5 0.0 copy-done.9
  12.5 0.0 copy-start.1
  12.5 0.0 copy-start.4
  12.5 0.0 copy-start.6
  12.6 2.2 %shard_map.83 = (bf16[256,256]{1,0:T(8,128)(2,1)S(1)}, bf16[128,128]{1,0:T(8,128)(2,1)S(1)}, bf16[64,64]{1,0:T(8,128)(2,1)S(1)}, bf16[3,8,256]{2,1,0:T(8,128)(2,...) custom-call(s32[3]{0:T(128)S(1)} %copy-done.9, ...), custom_call_target="tpu_custom_call" | custom-call | flops 1000000000 | bytes 1048576 | tf_op jit(solution)/shard_map/pallas_call | solution.py:244
  14.7 0.0 collective-permute-done.rim_in
  14.8 0.0 copy-done.1
  14.8 0.0 copy-done.4
  14.8 0.0 copy-done.6
  14.8 0.6 shard_map.84
  15.4 3.3 %collective-permute-start.1 = (bf16[256,448]{1,0:T(8,128)(2,1)S(1)}, bf16[256,448]{1,0:T(8,128)(2,1)S(1)}, u32[]{:S(2)}, u32[]{:S(2)}) collective-permute-start(bf16[256,448]{1,0:T(8,128)(2,1)S(1)} %get-tuple-element.26), channel_id=1, source_target_pairs={{0,1},{1,2},{2,3},{3,4},{4,5},{5,6},{6,7},{7,0},{8,9},{9,10},{10,1... | collective-permute-start | bytes 688136 | tf_op jit(solution)/shard_map/lon_right/ppermute | solution.py:266
  18.6 13.0 %collective-permute-start.2 = (bf16[256,448]{1,0:T(8,128)(2,1)S(1)}, bf16[256,448]{1,0:T(8,128)(2,1)S(1)}, u32[]{:S(2)}, u32[]{:S(2)}) collective-permute-start(bf16[256,448]{1,0:T(8,128)(2,1)S(1)} %get-tuple-element.27), channel_id=1, source_target_pairs={{1,0},{2,1},{3,2},{4,3},{5,4},{6,5},{7,6},{0,7},{9,8},{10,9},{11,1... | collective-permute-start | bytes 688136 | tf_op jit(solution)/shard_map/lon_left/ppermute | solution.py:268
  31.6 1.1 %shard_map.85.partial = f32[512,256]{1,0:T(8,128)S(1)} custom-call(bf16[1024,256]{1,0:T(8,128)(2,1)S(1)} %get-tuple-element.33.acr0, bf16[512,128]{1,0:T(8,128)(2,1)S(1)} %get-tuple-element.34.acr1, bf16[256,64]{1,0:T(8,128)(2,1)S(1)} %get-tuple-element.35.acr2, bf16[512,512]{1,0:T(8,128)(2,1)S(1)} %get-tuple-element.36.own0, ...), custom_call_target="tpu_custom_call" | custom-call | flops 1000000000 | bytes 1048576 | tf_op jit(solution)/shard_map/pallas_call | solution.py:270
  32.7 0.0 collective-permute-done.1.from_left
  32.7 0.0 collective-permute-done.2.from_right
  32.8 1.0 %shard_map.86 = bf16[512,256]{1,0:T(8,128)(2,1)S(1)} custom-call(bf16[256,448]{1,0:T(8,128)(2,1)S(1)} %collective-permute-done.1.from_left, bf16[256,448]{1,0:T(8,128)(2,1)S(1)} %collective-permute-done.2.from_right, bf16[512,256]{1,0:T(8,128)(2,1)S(1)} %get-tuple-element.28.side0, bf16[512,256]{1,0:T(8,128)(2,1)S(1)} %get-tuple-element.29.side1, ...), custom_call_target="tpu_custom_call" | custom-call | flops 1000000000 | bytes 1048576 | tf_op jit(solution)/shard_map/pallas_call | solution.py:276
  33.8 31.4 %all_to_all.5 = bf16[64,8,256]{2,1,0:T(8,128)(2,1)S(1)} all-to-all(bf16[64,8,256]{2,1,0:T(8,128)(2,1)S(1)} %bitcast.17), channel_id=1, replica_groups=mesh['mem'=64,'lat'=2,'lon'=8] {'mem'}, dimensions={0} | all-to-all | bytes 524288 | tf_op jit(solution)/shard_map/all_to_all | solution.py:285
  65.1 0.1 convert_reduce_fusion
  65.2 0.6 multiply_bitcast_fusion
  (1 shorter events, 0.0 us)
Async XLA Ops:
  0.0 1.0 %copy-start = (bf16[2,16,32,256]{3,2,1,0:T(8,128)(2,1)S(1)}, bf16[2,16,32,256]{3,2,1,0:T(8,128)(2,1)}, u32[]{:S(2)}) copy-start(bf16[2,16,32,256]{3,2,1,0:T(8,128)(2,1)} %param.9) | copy-start | bytes 1572868
  1.0 0.9 %copy-start.3 = (bf16[2,16,16,128]{3,2,1,0:T(8,128)(2,1)S(1)}, bf16[2,16,16,128]{3,2,1,0:T(8,128)(2,1)}, u32[]{:S(2)}) copy-start(bf16[2,16,16,128]{3,2,1,0:T(8,128)(2,1)} %param.10) | copy-start | bytes 393220
  1.9 0.8 %copy-start.5 = (bf16[2,16,8,64]{3,2,1,0:T(8,128)(2,1)S(1)}, bf16[2,16,8,64]{3,2,1,0:T(8,128)(2,1)}, u32[]{:S(2)}) copy-start(bf16[2,16,8,64]{3,2,1,0:T(8,128)(2,1)} %param.11) | copy-start | bytes 98308
  2.8 9.1 %copy-start.10 = (s32[384]{0:T(512)S(1)}, s32[384]{0:T(512)}, u32[]{:S(2)}) copy-start(s32[384]{0:T(512)} %param.13) | copy-start | bytes 4612
  2.8 9.1 %copy-start.2 = (bf16[2,16,32,256]{3,2,1,0:T(8,128)(2,1)S(1)}, bf16[2,16,32,256]{3,2,1,0:T(8,128)(2,1)}, u32[]{:S(2)}) copy-start(bf16[2,16,32,256]{3,2,1,0:T(8,128)(2,1)} %param.8) | copy-start | bytes 1572868
  2.8 9.1 %copy-start.7 = (bf16[3,16,16]{2,1,0:T(8,128)(2,1)S(1)}, bf16[3,16,16]{2,1,0:T(8,128)(2,1)}, u32[]{:S(2)}) copy-start(bf16[3,16,16]{2,1,0:T(8,128)(2,1)} %vertical.1) | copy-start | bytes 4612
  3.1 11.7 %collective-permute-start = (bf16[8,1792]{1,0:T(8,128)(2,1)S(1)}, bf16[8,1792]{1,0:T(8,128)(2,1)S(1)}, u32[]{:S(2)}, u32[]{:S(2)}) collective-permute-start(bf16[8,1792]{1,0:T(8,128)(2,1)S(1)} %shard_map.82), channel_id=1, source_target_pairs={{0,8},{8,0},{1,9},{9,1},{2,10},{10,2},{3,11},{11,3},{4,12},{12,4},... | collective-permute-start | bytes 86024 | tf_op jit(solution)/shard_map/lat_swap/ppermute | solution.py:237
  11.9 0.7 %copy-start.8 = (s32[192]{0:T(256)S(1)}, s32[192]{0:T(256)}, u32[]{:S(2)}) copy-start(s32[192]{0:T(256)} %param.14) | copy-start | bytes 2308
  11.9 0.7 %copy-start.9 = (s32[3]{0:T(128)S(1)}, s32[3]{0:T(128)}, u32[]{:S(2)}) copy-start(s32[3]{0:T(128)} %radii.1) | copy-start | bytes 40
  12.5 2.2 %copy-start.1 = (bf16[2,16,32,256]{3,2,1,0:T(8,128)(2,1)S(1)}, bf16[2,16,32,256]{3,2,1,0:T(8,128)(2,1)}, u32[]{:S(2)}) copy-start(bf16[2,16,32,256]{3,2,1,0:T(8,128)(2,1)} %param.9) | copy-start | bytes 1572868
  12.5 2.2 %copy-start.4 = (bf16[2,16,16,128]{3,2,1,0:T(8,128)(2,1)S(1)}, bf16[2,16,16,128]{3,2,1,0:T(8,128)(2,1)}, u32[]{:S(2)}) copy-start(bf16[2,16,16,128]{3,2,1,0:T(8,128)(2,1)} %param.10) | copy-start | bytes 393220
  12.5 2.2 %copy-start.6 = (bf16[2,16,8,64]{3,2,1,0:T(8,128)(2,1)S(1)}, bf16[2,16,8,64]{3,2,1,0:T(8,128)(2,1)}, u32[]{:S(2)}) copy-start(bf16[2,16,8,64]{3,2,1,0:T(8,128)(2,1)} %param.11) | copy-start | bytes 98308
  15.4 17.4 %collective-permute-start.1 = (bf16[256,448]{1,0:T(8,128)(2,1)S(1)}, bf16[256,448]{1,0:T(8,128)(2,1)S(1)}, u32[]{:S(2)}, u32[]{:S(2)}) collective-permute-start(bf16[256,448]{1,0:T(8,128)(2,1)S(1)} %get-tuple-element.26), channel_id=1, source_target_pairs={{0,1},{1,2},{2,3},{3,4},{4,5},{5,6},{6,7},{7,0},{8,9},{9,10},{10,1... | collective-permute-start | bytes 688136 | tf_op jit(solution)/shard_map/lon_right/ppermute | solution.py:266
  18.6 14.1 %collective-permute-start.2 = (bf16[256,448]{1,0:T(8,128)(2,1)S(1)}, bf16[256,448]{1,0:T(8,128)(2,1)S(1)}, u32[]{:S(2)}, u32[]{:S(2)}) collective-permute-start(bf16[256,448]{1,0:T(8,128)(2,1)S(1)} %get-tuple-element.27), channel_id=1, source_target_pairs={{1,0},{2,1},{3,2},{4,3},{5,4},{6,5},{7,6},{0,7},{9,8},{10,9},{11,1... | collective-permute-start | bytes 688136 | tf_op jit(solution)/shard_map/lon_left/ppermute | solution.py:268

commit v2 on v1

--- a/solution.py
+++ b/solution.py
@@ -40,13 +40,24 @@
     return (bell(offset, radius) / total).astype(B16)
 
 
-def edge_kernel(sizes, fine, mid, coarse, out):
+def edge_kernel(sizes, fine, mid, coarse, out, buf0, buf1, buf2, sems):
     low_half = lax.axis_index("lat") == 0
+    copies = []
+    for band, (ref, buf) in enumerate(zip((fine, mid, coarse), (buf0, buf1, buf2))):
+        width = buf.shape[1]
+        if width < ref.shape[1]:
+            first = pl.multiple_of(jnp.where(low_half, ref.shape[1] - width, 0), width)
+            ref = ref.at[:, pl.ds(first, width)]
+        copies.append(pltpu.make_async_copy(ref, buf, sems.at[band]))
+    for copy in copies:
+        copy.start()
     start = 0
-    for ref, (cells, rows) in zip((fine, mid, coarse), sizes):
-        base = jnp.where(low_half, rows - REACH, 0)
-        pick = (iota((REACH, rows), 1) == iota((REACH, rows), 0) + base).astype(B16)
-        out[:, start : start + cells] = dot(pick, ref[...], 1, 1).astype(B16)
+    for copy, buf in zip(copies, (buf0, buf1, buf2)):
+        cells, width = buf.shape
+        base = jnp.where(low_half, width - REACH, 0)
+        pick = (iota((REACH, width), 1) == iota((REACH, width), 0) + base).astype(B16)
+        copy.wait()
+        out[:, start : start + cells] = dot(pick, buf[...], 1, 1).astype(B16)
         start += cells
 
 
@@ -57,9 +68,12 @@
     vertical,
     mid_picks,
     coarse_picks,
-    row0,
-    row1,
-    row2,
+    fine,
+    mid,
+    coarse,
+    xr0,
+    xr1,
+    xr2,
     rim,
     own0,
     own1,
@@ -70,38 +84,46 @@
     res1,
     res2,
     spare,
+    buf0,
+    buf1,
+    buf2,
+    sems,
 ):
     lat = lax.axis_index("lat")
     lon = lax.axis_index("lon")
-    cols = sizes[0][0] // members.shape[0] * 32
-    bands = zip(FACTORS, sizes, (row0, row1, row2), (own0, own1, own2), (side0, side1, side2))
-    for band, (factor, (cells, rows), row_ref, own_ref, side_ref) in enumerate(bands):
+    cols = 32
+    copies = []
+    for band, (ref, buf) in enumerate(zip((fine, mid, coarse), (buf0, buf1, buf2))):
+        copies.append(pltpu.make_async_copy(ref, buf, sems.at[band]))
+        copies[band].start()
+    alongs = []
+    refs = zip((own0, own1, own2), (side0, side1, side2))
+    for band, (factor, (cells, rows), (own_ref, side_ref)) in enumerate(zip(FACTORS, sizes, refs)):
         radius = radii[band]
         total = bell_sum(radius)
         width = cols // factor
-        row_ref[...] = taps(iota((rows, rows), 0) - iota((rows, rows), 1), radius, total)
+        alongs.append(taps(iota((rows, rows), 0) - iota((rows, rows), 1), radius, total))
         base = jnp.where(lat == 0, rows, -REACH)
         shape = (REACH, rows)
         rim[band, :, :rows] = taps(iota(shape, 0) + base - iota(shape, 1), radius, total)
-        for ref, span in ((own_ref, width), (side_ref, REACH)):
+        reach_cols = factor * REACH
+        parts = (
+            (own_ref, 0, width, cols, 0, 0),
+            (side_ref, 0, REACH, reach_cols, 0, -REACH),
+            (side_ref, LEV * REACH, REACH, reach_cols, cols - reach_cols, width),
+        )
+        for to, at, span, count, first, shift in parts:
             lanes = LEV * span
-            shape = (cols, lanes)
-            place = iota(shape, 1) % span
-            target = iota(shape, 0) // factor
+            place = iota((count, lanes), 1) % span + shift
+            target = (iota((count, lanes), 0) + first) // factor
+            pattern = taps(place - target, radius, total).astype(F32)
             level = (iota((LEV, lanes), 0) == iota((LEV, lanes), 1) // span).astype(B16)
             spread = dot(vertical[band], level)
-            if span == width and ref is own_ref:
-                parts = ((0, taps(place - target, radius, total)),)
-            else:
-                parts = (
-                    (0, taps(place - REACH - target, radius, total)),
-                    (lanes, taps(place + width - target, radius, total)),
-                )
-            for at, pattern in parts:
-                pattern = pattern.astype(F32)
-                for k in range(LEV):
-                    block = (spread[k : k + 1] * pattern).astype(B16)
-                    ref[k * cols : (k + 1) * cols, at : at + lanes] = block
+            for k in range(LEV):
+                to[k * count : (k + 1) * count, at : at + lanes] = (spread[k : k + 1] * pattern).astype(B16)
+    for copy, buf, along, xr in zip(copies, (buf0, buf1, buf2), alongs, (xr0, xr1, xr2)):
+        copy.wait()
+        xr[...] = dot(buf[...], along)
     full_rows = sizes[0][1]
     block = 8 * cols
     for factor, picks, out in ((2, mid_picks, res1), (4, coarse_picks, res2)):
@@ -129,25 +151,27 @@
             out[at] = dot(col_pick, by_rows).astype(B16)
 
 
-def rows_kernel(sizes, fine, mid, coarse, rim_in, row0, row1, row2, rim, out0, out1, out2, right, left):
+def rows_kernel(sizes, rim_in, xr0, xr1, xr2, rim, out0, out1, out2, odd, even):
+    sends_left_first = lax.axis_index("lon") % 2 == 0
     start = 0
     lane = 0
-    bands = zip(FACTORS, sizes, (fine, mid, coarse), (row0, row1, row2), (out0, out1, out2))
-    for band, (factor, (cells, rows), ref, row_ref, out) in enumerate(bands):
+    bands = zip(FACTORS, sizes, (xr0, xr1, xr2), (out0, out1, out2))
+    for band, (factor, (cells, rows), xr, out) in enumerate(bands):
         width = 32 // factor
-        matrix = row_ref[...]
         edge = rim[band, :, :rows]
         chunk = 128
         groups = chunk // width
         for part in range(cells // chunk):
             at = slice(part * chunk, (part + 1) * chunk)
             arrived = rim_in[:, start + part * chunk : start + (part + 1) * chunk]
-            across = dot(ref[at], matrix) + dot(arrived, edge, 0, 0)
+            across = xr[at] + dot(arrived, edge, 0, 0)
             out[at] = across.astype(B16)
             cut = across.reshape(groups, width, rows)
+            right = cut[:, width - REACH :].reshape(-1, rows)
+            left = cut[:, :REACH].reshape(-1, rows)
             to = slice(part * groups * REACH, (part + 1) * groups * REACH)
-            right[to, lane : lane + rows] = cut[:, width - REACH :].reshape(-1, rows).astype(B16)
-            left[to, lane : lane + rows] = cut[:, :REACH].reshape(-1, rows).astype(B16)
+            odd[to, lane : lane + rows] = jnp.where(sends_left_first, left, right).astype(B16)
+            even[to, lane : lane + rows] = jnp.where(sends_left_first, right, left).astype(B16)
         start += cells
         lane += rows
 
@@ -173,26 +197,39 @@
             first = False
 
 
-def side_kernel(sizes, from_left, from_right, side0, side1, side2, members, res1, res2, partial, out, total):
+def side_kernel(sizes, odd, even, side0, side1, side2, members, res1, res2, partial, out, total):
+    left_is_odd = lax.axis_index("lon") % 2 == 0
+    total[...] = partial[...].reshape(total.shape)
+    half = odd.shape[0] // 2
+    size = members.shape[0] // 2
+    cols = total.shape[1]
     lane = 0
-    total[...] = partial[...]
     bands = zip(FACTORS, sizes, (side0, side1, side2), (members, res1, res2))
     for factor, (cells, rows), side, res in bands:
-        half = from_left.shape[0] // 2
-        size = res.shape[0] // 2
+        count = factor * REACH
         for m in range(2):
             at = slice(m * half, (m + 1) * half)
-            both = jnp.concatenate(
-                [from_left[at, lane : lane + rows], from_right[at, lane : lane + rows]], axis=0
-            )
-            local = dot(side[...], widen(both, factor))
-            total[...] += local * res[m * size : (m + 1) * size].astype(F32)
+            one = odd[at, lane : lane + rows]
+            two = even[at, lane : lane + rows]
+            left = jnp.where(left_is_odd, one, two)
+            right = jnp.where(left_is_odd, two, one)
+            weight = res[m * size : (m + 1) * size].reshape(total.shape)
+            if count == cols:
+                local = dot(side[...], widen(jnp.concatenate([left, right], axis=0), factor))
+                total[...] += local.reshape(total.shape) * weight.astype(F32)
+                continue
+            for begin, first, came in ((0, 0, left), (half, cols - count, right)):
+                local = dot(side[:, begin : begin + half], widen(came, factor))
+                where = slice(first, first + count)
+                local = local.reshape(LEV, count, -1)
+                total[:, where] += local * weight[:, where].astype(F32)
         lane += rows
-    out[...] = total[...].astype(B16)
+    out[...] = total[...].reshape(out.shape).astype(B16)
 
 
 VMEM = pl.BlockSpec(memory_space=pltpu.VMEM)
 SMEM = pl.BlockSpec(memory_space=pltpu.SMEM)
+HBM = pl.BlockSpec(memory_space=pltpu.HBM)
 
 
 def call(kernel, outs, in_specs, scratch=(), flops=0, limit=24):
@@ -231,24 +268,28 @@
     out_cells = fine_cells // 2
 
     edge = call(
-        functools.partial(edge_kernel, sizes), [((REACH, all_cells), B16)], [VMEM] * 3, flops=10**7
-    )(*controls)
+        functools.partial(edge_kernel, sizes),
+        [((REACH, all_cells), B16)],
+        [HBM] * 3,
+        [pltpu.VMEM((cells, min(rows, 128)), B16) for cells, rows in sizes] + [pltpu.SemaphoreType.DMA((3,))],
+        flops=10**7,
+    )(*[pltpu.with_memory_space_constraint(c, pltpu.HBM) for c in controls])
     with jax.named_scope("lat_swap"):
         arrived = lax.ppermute(edge, "lat", [(0, 1), (1, 0)])
 
-    outs = [((rows, rows), B16) for _, rows in sizes]
+    outs = [(s, F32) for s in sizes]
     outs += [((3, REACH, fine_rows), B16)]
     outs += [((out_cells, cells // 2), B16) for cells, _ in sizes]
-    outs += [((out_cells, 2 * LEV * REACH), B16)] * 3
+    outs += [((LEV * factor * REACH, 2 * LEV * REACH), B16) for factor in FACTORS]
     outs += [((fine_cells, fine_rows), B16)] * 2
     prep = call(
         functools.partial(prep_kernel, sizes),
         outs,
-        [SMEM] + [VMEM] * 4,
-        [pltpu.VMEM((256, 256), B16)],
+        [SMEM] + [VMEM] * 4 + [HBM] * 3,
+        [pltpu.VMEM((256, 256), B16)] + [pltpu.VMEM(s, B16) for s in sizes] + [pltpu.SemaphoreType.DMA((3,))],
         flops=10**9,
-    )(band_radii, members, vertical, mid_picks[None], coarse_picks[None])
-    rows = prep[0:3]
+    )(band_radii, members, vertical, mid_picks[None], coarse_picks[None], *controls)
+    filtered = prep[0:3]
     rim = prep[3]
     own = prep[4:7]
     side = prep[7:10]
@@ -257,15 +298,17 @@
     filtered = call(
         functools.partial(rows_kernel, sizes),
         [(s, B16) for s in sizes] + [((held * REACH, all_rows), B16)] * 2,
-        [VMEM] * 8,
+        [VMEM] * 5,
         flops=2 * 10**8,
-    )(*controls, arrived, *rows, rim)
+    )(arrived, *filtered, rim)
     across = filtered[0:3]
     count = lax.axis_size("lon")
-    with jax.named_scope("lon_right"):
-        from_left = lax.ppermute(filtered[3], "lon", [(i, (i + 1) % count) for i in range(count)])
-    with jax.named_scope("lon_left"):
-        from_right = lax.ppermute(filtered[4], "lon", [((i + 1) % count, i) for i in range(count)])
+    pairs = [(i, (i + 1) % count) for i in range(1, count, 2)]
+    with jax.named_scope("lon_odd"):
+        odd = lax.ppermute(filtered[3], "lon", pairs + [(j, i) for i, j in pairs])
+    pairs = [(i, i + 1) for i in range(0, count, 2)]
+    with jax.named_scope("lon_even"):
+        even = lax.ppermute(filtered[4], "lon", pairs + [(j, i) for i, j in pairs])
 
     partial = call(
         functools.partial(own_kernel, sizes),
@@ -277,9 +320,9 @@
         functools.partial(side_kernel, sizes),
         [((out_cells, fine_rows), B16)],
         [VMEM] * 9,
-        [pltpu.VMEM((out_cells, fine_rows), F32)],
+        [pltpu.VMEM((LEV, out_cells // LEV, fine_rows), F32)],
         flops=10**9,
-    )(from_left, from_right, *side, members, *res, partial)
+    )(odd, even, *side, members, *res, partial)
 
     blocks = field.reshape(devices, out_cells // devices, fine_rows)
     blocks = lax.all_to_all(blocks, "mem", split_axis=0, concat_axis=0, tiled=True)

time: 66.2 us -> 63.5 us (0.959)
  the two profiles are of different devices: /device:TPU:1 before, /device:TPU:2 now
where the time goes in v2:
time: 63.5 us; the launch traced here: 63.2 us
  blocking collectives  35.5 us (56%)
  starting transfers between devices  12.9 us (20%)
  Pallas kernels  7.39 us (12%)
  waiting for transfers between devices  4.86 us (8%)
  local copies, waits for them, and re-layouts  1.69 us (3%)
  other arithmetic  0.67 us (1%)
    all_to_all x1, blocking collectives, on_device(): lax.all_to_all(blocks, 'mem', split_axis=0, concat_axis=0, tiled=True)  35.5 us
    ppermute x1, starting transfers between devices, on_device(): arrived = lax.ppermute(edge, 'lat', [(0, 1), (1, 0)])  8.19 us
    ppermute x1, waiting for transfers between devices, on_device(): odd = lax.ppermute(filtered[3], 'lon', pairs + [(j, i) for i, j in pairs])  4.85 us
    pallas_call x1, Pallas kernels, on_device(): call(functools.partial(prep_kernel, sizes), outs, [SMEM] + [VMEM] * 4 + [...  3.22 us
    ppermute x1, starting transfers between devices, on_device(): even = lax.ppermute(filtered[4], 'lon', pairs + [(j, i) for i, j in pairs])  2.41 us
    ppermute x1, starting transfers between devices, on_device(): odd = lax.ppermute(filtered[3], 'lon', pairs + [(j, i) for i, j in pairs])  2.3 us
    unnamed x16, local copies, waits for them, and re-layouts  1.69 us
    pallas_call x1, Pallas kernels, on_device(): call(functools.partial(edge_kernel, sizes), [((REACH, all_cells), B16)],...  1.54 us
  transfers between devices with their start and end apart: 3, of which 1 were waited for; matrix products, arithmetic and copies ran while one was open for 0% of the time, Pallas kernels for 7%

profile of v2, /device:TPU:2, one launch (start us, length us, event | category | flops | bytes accessed | tf_op | source)
XLA Modules:
  0.0 63.2 jit_solution(7604161135705262266)
XLA Ops:
  0.0 0.0 copy-start
  0.0 0.0 copy-start.7
  0.0 0.0 copy-start.2
  0.0 0.0 copy-start.3
  0.0 0.0 copy-start.4
  0.0 1.5 %shard_map.82 = bf16[8,1792]{1,0:T(8,128)(2,1)S(1)} custom-call(bf16[1024,256]{1,0:T(8,128)(2,1)} %bitcast.11, bf16[512,128]{1,0:T(8,128)(2,1)} %bitcast.14, bf16[256,64]{1,0:T(8,128)(2,1)} %bitcast.16), custom_call_target="tpu_custom_call" | custom-call | flops 10000000 | bytes 1048576 | tf_op jit(solution)/shard_map/pallas_call | solution.py:270
  1.6 8.2 %collective-permute-start = (bf16[8,1792]{1,0:T(8,128)(2,1)S(1)}, bf16[8,1792]{1,0:T(8,128)(2,1)S(1)}, u32[]{:S(2)}, u32[]{:S(2)}) collective-permute-start(bf16[8,1792]{1,0:T(8,128)(2,1)S(1)} %shard_map.82), channel_id=1, source_target_pairs={{0,8},{8,0},{1,9},{9,1},{2,10},{10,2},{3,11},{11,3},{4,12},{12,4},... | collective-permute-start | bytes 86024 | tf_op jit(solution)/shard_map/lat_swap/ppermute | solution.py:278
  9.8 0.0 copy-done.7
  9.8 0.0 copy-start.5
  9.8 0.0 copy-start.6
  9.8 0.0 copy-done
  9.8 0.0 copy-done.2
  9.8 0.0 copy-done.3
  9.8 0.0 copy-done.4
  9.9 0.6 copy-done.5
  10.5 0.0 copy-done.6
  10.5 0.0 copy-start.1
  10.5 1.0 %copy-done.1 = bf16[2,16,32,256]{3,2,1,0:T(8,128)(2,1)S(1)} copy-done((bf16[2,16,32,256]{3,2,1,0:T(8,128)(2,1)S(1)}, bf16[2,16,32,256]{3,2,1,0:T(8,128)(2,1)}, u32[]{:S(2)}) %copy-start.1) | copy-done | bytes 524312
  11.5 3.2 %shard_map.83 = (f32[1024,256]{1,0:T(8,128)S(1)}, f32[512,128]{1,0:T(8,128)S(1)}, f32[256,64]{1,0:T(8,128)S(1)}, bf16[3,8,256]{2,1,0:T(8,128)(2,1)S(1)}, bf16[51...) custom-call(s32[3]{0:T(128)S(1)} %copy-done.6, ...), custom_call_target="tpu_custom_call" | custom-call | flops 1000000000 | bytes 1048576 | tf_op jit(solution)/shard_map/pallas_call | solution.py:285
  14.7 0.0 collective-permute-done.rim_in
  14.8 0.4 shard_map.84
  15.2 2.3 %collective-permute-start.1 = (bf16[256,448]{1,0:T(8,128)(2,1)S(1)}, bf16[256,448]{1,0:T(8,128)(2,1)S(1)}, u32[]{:S(2)}, u32[]{:S(2)}) collective-permute-start(bf16[256,448]{1,0:T(8,128)(2,1)S(1)} %get-tuple-element.26), channel_id=1, source_target_pairs={{1,2},{3,4},{5,6},{7,0},{2,1},{4,3},{6,5},{0,7},{9,10},{11,12},{13... | collective-permute-start | bytes 688136 | tf_op jit(solution)/shard_map/lon_odd/ppermute | solution.py:308
  17.5 2.4 %collective-permute-start.2 = (bf16[256,448]{1,0:T(8,128)(2,1)S(1)}, bf16[256,448]{1,0:T(8,128)(2,1)S(1)}, u32[]{:S(2)}, u32[]{:S(2)}) collective-permute-start(bf16[256,448]{1,0:T(8,128)(2,1)S(1)} %get-tuple-element.27), channel_id=1, source_target_pairs={{0,1},{2,3},{4,5},{6,7},{1,0},{3,2},{5,4},{7,6},{8,9},{10,11},{12,... | collective-permute-start | bytes 688136 | tf_op jit(solution)/shard_map/lon_even/ppermute | solution.py:311
  19.9 1.1 %shard_map.85.partial = f32[512,256]{1,0:T(8,128)S(1)} custom-call(bf16[1024,256]{1,0:T(8,128)(2,1)S(1)} %get-tuple-element.33.acr0, bf16[512,128]{1,0:T(8,128)(2,1)S(1)} %get-tuple-element.34.acr1, bf16[256,64]{1,0:T(8,128)(2,1)S(1)} %get-tuple-element.35.acr2, bf16[512,512]{1,0:T(8,128)(2,1)S(1)} %get-tuple-element.36.own0, ...), custom_call_target="tpu_custom_call" | custom-call | flops 1000000000 | bytes 1048576 | tf_op jit(solution)/shard_map/pallas_call | solution.py:313
  21.0 4.9 %collective-permute-done.1.odd = bf16[256,448]{1,0:T(8,128)(2,1)S(1)} collective-permute-done((bf16[256,448]{1,0:T(8,128)(2,1)S(1)}, bf16[256,448]{1,0:T(8,128)(2,1)S(1)}, u32[]{:S(2)}, u32[]{:S(2)}) %collective-permute-start.1) | collective-permute-done | bytes 229408 | tf_op jit(solution)/shard_map/lon_odd/ppermute | solution.py:308
  25.8 0.0 collective-permute-done.2.even
  25.8 1.1 %shard_map.86 = bf16[512,256]{1,0:T(8,128)(2,1)S(1)} custom-call(bf16[256,448]{1,0:T(8,128)(2,1)S(1)} %collective-permute-done.1.odd, bf16[256,448]{1,0:T(8,128)(2,1)S(1)} %collective-permute-done.2.even, bf16[128,256]{1,0:T(8,128)(2,1)S(1)} %get-tuple-element.28.side0, bf16[256,256]{1,0:T(8,128)(2,1)S(1)} %get-tuple-element.29.side1, ...), custom_call_target="tpu_custom_call" | custom-call | flops 1000000000 | bytes 1048576 | tf_op jit(solution)/shard_map/pallas_call | solution.py:319
  27.0 35.5 %all_to_all.5 = bf16[64,8,256]{2,1,0:T(8,128)(2,1)S(1)} all-to-all(bf16[64,8,256]{2,1,0:T(8,128)(2,1)S(1)} %bitcast.13), channel_id=1, replica_groups=mesh['mem'=64,'lat'=2,'lon'=8] {'mem'}, dimensions={0} | all-to-all | bytes 524288 | tf_op jit(solution)/shard_map/all_to_all | solution.py:328
  62.5 0.1 convert_reduce_fusion
  62.6 0.6 multiply_bitcast_fusion
  (1 shorter events, 0.0 us)
Async XLA Ops:
  0.0 9.8 %copy-start = (bf16[2,16,32,256]{3,2,1,0:T(8,128)(2,1)S(1)}, bf16[2,16,32,256]{3,2,1,0:T(8,128)(2,1)}, u32[]{:S(2)}) copy-start(bf16[2,16,32,256]{3,2,1,0:T(8,128)(2,1)} %param.8) | copy-start | bytes 1572868
  0.0 9.8 %copy-start.7 = (s32[384]{0:T(512)S(1)}, s32[384]{0:T(512)}, u32[]{:S(2)}) copy-start(s32[384]{0:T(512)} %param.13) | copy-start | bytes 4612
  0.0 9.8 %copy-start.2 = (bf16[2,16,16,128]{3,2,1,0:T(8,128)(2,1)S(1)}, bf16[2,16,16,128]{3,2,1,0:T(8,128)(2,1)}, u32[]{:S(2)}) copy-start(bf16[2,16,16,128]{3,2,1,0:T(8,128)(2,1)} %param.10) | copy-start | bytes 393220
  0.0 9.8 %copy-start.3 = (bf16[2,16,8,64]{3,2,1,0:T(8,128)(2,1)S(1)}, bf16[2,16,8,64]{3,2,1,0:T(8,128)(2,1)}, u32[]{:S(2)}) copy-start(bf16[2,16,8,64]{3,2,1,0:T(8,128)(2,1)} %param.11) | copy-start | bytes 98308
  0.0 9.8 %copy-start.4 = (bf16[3,16,16]{2,1,0:T(8,128)(2,1)S(1)}, bf16[3,16,16]{2,1,0:T(8,128)(2,1)}, u32[]{:S(2)}) copy-start(bf16[3,16,16]{2,1,0:T(8,128)(2,1)} %vertical.1) | copy-start | bytes 4612
  1.6 13.2 %collective-permute-start = (bf16[8,1792]{1,0:T(8,128)(2,1)S(1)}, bf16[8,1792]{1,0:T(8,128)(2,1)S(1)}, u32[]{:S(2)}, u32[]{:S(2)}) collective-permute-start(bf16[8,1792]{1,0:T(8,128)(2,1)S(1)} %shard_map.82), channel_id=1, source_target_pairs={{0,8},{8,0},{1,9},{9,1},{2,10},{10,2},{3,11},{11,3},{4,12},{12,4},... | collective-permute-start | bytes 86024 | tf_op jit(solution)/shard_map/lat_swap/ppermute | solution.py:278
  9.8 0.7 %copy-start.5 = (s32[192]{0:T(256)S(1)}, s32[192]{0:T(256)}, u32[]{:S(2)}) copy-start(s32[192]{0:T(256)} %param.14) | copy-start | bytes 2308
  9.8 0.7 %copy-start.6 = (s32[3]{0:T(128)S(1)}, s32[3]{0:T(128)}, u32[]{:S(2)}) copy-start(s32[3]{0:T(128)} %radii.1) | copy-start | bytes 40
  10.5 1.0 %copy-start.1 = (bf16[2,16,32,256]{3,2,1,0:T(8,128)(2,1)S(1)}, bf16[2,16,32,256]{3,2,1,0:T(8,128)(2,1)}, u32[]{:S(2)}) copy-start(bf16[2,16,32,256]{3,2,1,0:T(8,128)(2,1)} %param.9) | copy-start | bytes 1572868
  15.2 10.7 %collective-permute-start.1 = (bf16[256,448]{1,0:T(8,128)(2,1)S(1)}, bf16[256,448]{1,0:T(8,128)(2,1)S(1)}, u32[]{:S(2)}, u32[]{:S(2)}) collective-permute-start(bf16[256,448]{1,0:T(8,128)(2,1)S(1)} %get-tuple-element.26), channel_id=1, source_target_pairs={{1,2},{3,4},{5,6},{7,0},{2,1},{4,3},{6,5},{0,7},{9,10},{11,12},{13... | collective-permute-start | bytes 688136 | tf_op jit(solution)/shard_map/lon_odd/ppermute | solution.py:308
  17.5 8.4 %collective-permute-start.2 = (bf16[256,448]{1,0:T(8,128)(2,1)S(1)}, bf16[256,448]{1,0:T(8,128)(2,1)S(1)}, u32[]{:S(2)}, u32[]{:S(2)}) collective-permute-start(bf16[256,448]{1,0:T(8,128)(2,1)S(1)} %get-tuple-element.27), channel_id=1, source_target_pairs={{0,1},{2,3},{4,5},{6,7},{1,0},{3,2},{5,4},{7,6},{8,9},{10,11},{12,... | collective-permute-start | bytes 688136 | tf_op jit(solution)/shard_map/lon_even/ppermute | solution.py:311

commit v3 on v2

v3 whole, which is shorter than its diff:
```python
import functools
import math

import jax
import jax.numpy as jnp
from jax import lax
from jax.experimental import pallas as pl
from jax.experimental.pallas import tpu as pltpu
from jax.sharding import PartitionSpec as P


REACH = 8
LEV = 16
FACTORS = (1, 2, 4)
B16 = jnp.bfloat16
F32 = jnp.float32


def iota(shape, dim):
    return lax.broadcasted_iota(jnp.int32, shape, dim)


def dot(a, b, ca=1, cb=0):
    return lax.dot_general(a, b, (((ca,), (cb,)), ((), ())), preferred_element_type=F32)


def bell(offset, radius):
    wide = offset.astype(F32)
    reach_now = jnp.broadcast_to(radius.astype(F32), wide.shape)
    raw = jnp.exp(-0.5 * jnp.square(wide / (0.5 * reach_now)))
    return jnp.where(jnp.abs(wide) <= reach_now, raw, 0.0)


def bell_sum(radius):
    lanes = iota((8, 128), 1)
    raw = jnp.where(lanes <= 2 * REACH, bell(lanes - REACH, radius), 0.0)
    return jnp.sum(raw, axis=1, keepdims=True)[0:1]


def taps(offset, radius, total):
    return (bell(offset, radius) / total).astype(B16)


def edge_kernel(fine, mid, coarse, out, odd, even, buf0, buf1, buf2, buf3, sems):
    low_half = lax.axis_index("lat") == 0
    left_is_odd = lax.axis_index("lon") % 2 == 0
    copies = []

    def begin(source, to):
        copies.append(pltpu.make_async_copy(source, to, sems.at[len(copies)]))
        copies[-1].start()

    held = fine.shape[0]
    first = pl.multiple_of(jnp.where(low_half, fine.shape[2] - 128, 0), 128)
    for ref, buf, lanes in ((coarse, buf2, None), (mid, buf1, None), (fine, buf0, first)):
        for group in range(ref.shape[1] // REACH):
            source = ref.at[:, group * REACH : (group + 1) * REACH]
            if lanes is not None:
                source = ref.at[:, group * REACH : (group + 1) * REACH, pl.ds(lanes, 128)]
            begin(source, buf.at[group])
    for_rows = len(copies)
    begin(coarse, buf3)
    for to, goes_left in ((odd, left_is_odd), (even, jnp.logical_not(left_is_odd))):
        at = 0
        for ref in (fine, mid):
            column = pl.multiple_of(jnp.where(goes_left, 0, ref.shape[1] - REACH), REACH)
            for lane in range(0, ref.shape[2], 128):
                begin(ref.at[:, pl.ds(column, REACH), lane : lane + 128], to.at[at : at + held])
                at += held
    for copy in copies[:for_rows]:
        copy.wait()
    start = 0
    for buf in (buf0, buf1, buf2):
        width = buf.shape[-1]
        base = jnp.where(low_half, width - REACH, 0)
        pick = (iota((REACH, width), 1) == iota((REACH, width), 0) + base).astype(B16)
        cells = buf.shape[0] * held * REACH
        rows = buf[...].astype(F32).reshape(cells, width).astype(B16)
        out[:, start : start + cells] = dot(pick, rows, 1, 1).astype(B16)
        start += cells
    copies[for_rows].wait()
    for to in (odd, even):
        to[3 * held :, :, : buf3.shape[2]] = buf3[...]
    for copy in copies[for_rows + 1 :]:
        copy.wait()


def prep_kernel(
    sizes,
    radii,
    members,
    vertical,
    mid_picks,
    coarse_picks,
    fine,
    mid,
    coarse,
    xr0,
    xr1,
    xr2,
    row0,
    row1,
    row2,
    rim,
    own0,
    own1,
    own2,
    side0,
    side1,
    side2,
    res1,
    res2,
    spare,
    buf0,
    buf1,
    buf2,
    sems,
):
    lat = lax.axis_index("lat")
    lon = lax.axis_index("lon")
    cols = 32
    copies = []
    for band, (ref, buf) in enumerate(zip((fine, mid, coarse), (buf0, buf1, buf2))):
        copies.append(pltpu.make_async_copy(ref, buf, sems.at[band]))
        copies[band].start()
    refs = zip((row0, row1, row2), (own0, own1, own2), (side0, side1, side2))
    for band, (factor, (cells, rows), (row_ref, own_ref, side_ref)) in enumerate(zip(FACTORS, sizes, refs)):
        radius = radii[band]
        total = bell_sum(radius)
        width = cols // factor
        shape = (rows, rows * factor)
        row_ref[...] = taps(iota(shape, 0) - iota(shape, 1) // factor, radius, total)
        base = jnp.where(lat == 0, rows, -REACH)
        shape = (REACH, rows * factor)
        rim[band] = taps(iota(shape, 0) + base - iota(shape, 1) // factor, radius, total)
        reach_cols = factor * REACH
        parts = (
            (own_ref, 0, width, cols, 0, 0),
            (side_ref, 0, REACH, reach_cols, 0, -REACH),
            (side_ref, LEV * REACH, REACH, reach_cols, cols - reach_cols, width),
        )
        for to, at, span, count, first, shift in parts:
            lanes = LEV * span
            place = iota((count, lanes), 1) % span + shift
            target = (iota((count, lanes), 0) + first) // factor
            pattern = taps(place - target, radius, total).astype(F32)
            level = (iota((LEV, lanes), 0) == iota((LEV, lanes), 1) // span).astype(B16)
            spread = dot(vertical[band], level)
            for k in range(LEV):
                to[k * count : (k + 1) * count, at : at + lanes] = (spread[k : k + 1] * pattern).astype(B16)
    for copy, buf, row_ref, xr in zip(copies, (buf0, buf1, buf2), (row0, row1, row2), (xr0, xr1, xr2)):
        copy.wait()
        xr[...] = dot(buf[...], row_ref[...])
    full_rows = sizes[0][1]
    block = 8 * cols
    for factor, picks, out in ((2, mid_picks, res1), (4, coarse_picks, res2)):
        n = picks.shape[1]
        rows = full_rows // factor
        width = cols // factor
        values = jnp.broadcast_to(picks[...].astype(F32), (8, n)).astype(B16)
        shape = (n, full_rows)
        hot = (iota(shape, 0) == lat * rows + iota(shape, 1) // factor).astype(B16)
        chosen = dot(values, hot)[0:1]
        shape = (full_rows, full_rows)
        wanted = (factor * (iota((1, full_rows), 1) // factor)).astype(F32) + chosen
        row_pick = (iota(shape, 0).astype(F32) == wanted).astype(B16)
        shape = (cols, n)
        hot = (iota(shape, 1) == 2 * rows + lon * width + iota(shape, 0) // factor).astype(B16)
        chosen = dot(hot, values, 1, 1)[:, 0:1]
        wanted = (factor * (iota((cols, 1), 0) // factor)).astype(F32) + chosen
        lanes = iota((cols, block), 1).astype(F32)
        for k in range(8):
            spare[k * cols : (k + 1) * cols] = (lanes == wanted + F32(k * cols)).astype(B16)
        col_pick = spare[...]
        for part in range(members.shape[0] // block):
            at = slice(part * block, (part + 1) * block)
            by_rows = dot(members[at], row_pick).astype(B16)
            out[at] = dot(col_pick, by_rows).astype(B16)


def forward_kernel(sizes, rim_in, main, odd, even):
    left_is_odd = lax.axis_index("lon") % 2 == 0
    start = 0
    span = main.shape[0] // 4 * REACH
    even[: main.shape[0]] = main[...]
    for band, (cells, rows) in enumerate(sizes):
        for part in range(0, span, 128):
            left = rim_in[:, start + part : start + part + 128]
            right = rim_in[:, start + cells - span + part : start + cells - span + part + 128]
            at = band * span + part
            odd[:, at : at + 128] = jnp.where(left_is_odd, left, right)
            even[main.shape[0] + at // 128] = jnp.where(left_is_odd, right, left)
        start += cells


def own_kernel(sizes, rim_in, xr0, xr1, xr2, rim, own0, own1, own2, members, res1, res2, out):
    first = True
    start = 0
    held = 2 * LEV
    bands = zip(FACTORS, sizes, (xr0, xr1, xr2), (own0, own1, own2), (members, res1, res2))
    for band, (factor, (cells, rows), xr, own, res) in enumerate(bands):
        width = cells // held
        size = res.shape[0] // 2
        edge = rim[band]
        span = LEV * REACH
        for m in range(2):
            sums = xr[m * cells // 2 : (m + 1) * cells // 2].reshape(LEV, width, -1)
            parts = []
            for group in range(width // REACH):
                at = start + (2 * group + m) * span
                parts.append(dot(rim_in[:, at : at + span], edge, 0, 0).reshape(LEV, REACH, -1))
            sums = sums + (parts[0] if len(parts) == 1 else jnp.concatenate(parts, axis=1))
            across = sums.reshape(LEV * width, -1).astype(B16)
            product = dot(own[...], across) * res[m * size : (m + 1) * size].astype(F32)
            out[...] = product if first else out[...] + product
            first = False
        start += cells


def side_kernel(
    sizes,
    odd,
    odd_rim,
    even,
    even_rim,
    row0,
    row1,
    row2,
    rim,
    side0,
    side1,
    side2,
    members,
    res1,
    res2,
    partial,
    out,
    total,
):
    left_is_odd = lax.axis_index("lon") % 2 == 0
    size = members.shape[0] // 2
    cols = total.shape[1]
    span = 2 * LEV * REACH
    half = span // 2
    tiles = even_rim.shape[0] - 6
    at = 3 * span
    order = []
    bands = zip(FACTORS, sizes, (row0, row1, row2), (side0, side1, side2), (members, res1, res2))
    for band, (factor, (cells, rows), row_ref, side, res) in reversed(list(enumerate(bands))):
        both = [0.0, 0.0]
        for lane in reversed(range(0, rows, 128)):
            wide = min(rows, 128)
            one = odd[at : at + span, :wide]
            two = even[at : at + span, :wide]
            at -= span
            matrix = row_ref[lane : lane + wide]
            both[0] += dot(jnp.where(left_is_odd, one, two), matrix)
            both[1] += dot(jnp.where(left_is_odd, two, one), matrix)
        for m in range(2):
            one = odd_rim[:, band * span + m * half : band * span + (m + 1) * half]
            two = even_rim[tiles + 2 * band + m]
            edges = (jnp.where(left_is_odd, one, two), jnp.where(left_is_odd, two, one))
            left, right = [
                (main[m * half : (m + 1) * half] + dot(edge, rim[band], 0, 0)).astype(B16)
                for main, edge in zip(both, edges)
            ]
            order.append((factor, side, res, m, left, right))
    order = order[:1] + order[2:] + order[1:2]
    shape = total.shape
    for step, (factor, side, res, m, left, right) in enumerate(order):
        weight = res[m * size : (m + 1) * size]
        count = factor * REACH
        if count == cols:
            product = dot(side[...], jnp.concatenate([left, right], axis=0)) * weight.astype(F32)
            if step == 0:
                total[...] = (partial[...] + product).reshape(shape)
            else:
                out[...] = (total[...].reshape(out.shape) + product).astype(B16)
            continue
        weight = weight.reshape(shape)
        for begin, first, came in ((0, 0, left), (half, cols - count, right)):
            local = dot(side[:, begin : begin + half], came).reshape(LEV, count, -1)
            where = slice(first, first + count)
            total[:, where] += local * weight[:, where].astype(F32)


VMEM = pl.BlockSpec(memory_space=pltpu.VMEM)
SMEM = pl.BlockSpec(memory_space=pltpu.SMEM)
HBM = pl.BlockSpec(memory_space=pltpu.HBM)


def call(*args, **kwargs):
    def run(*operands):
        return kernel_call(*args, **kwargs)(*operands)

    return run


def kernel_call(kernel, outs, in_specs, scratch=(), flops=0, limit=24):
    shapes = [jax.ShapeDtypeStruct(shape, kind) for shape, kind in outs]
    many = len(shapes) > 1
    return pl.pallas_call(
        kernel,
        out_shape=shapes if many else shapes[0],
        in_specs=in_specs,
        out_specs=[VMEM] * len(shapes) if many else VMEM,
        scratch_shapes=scratch,
        compiler_params=pltpu.CompilerParams(vmem_limit_bytes=limit << 20),
        cost_estimate=pl.CostEstimate(flops=flops, bytes_accessed=1 << 20, transcendentals=0),
    )


def on_device(
    members,
    control_fine,
    control_mid,
    control_coarse,
    vertical,
    mid_picks,
    coarse_picks,
    band_radii,
):
    devices = lax.axis_size("mem")
    member_total = members.shape[0] * devices
    held = members.shape[0] * LEV
    raw = [
        pltpu.with_memory_space_constraint(c.reshape(held, c.shape[2], c.shape[3]), pltpu.HBM)
        for c in (control_fine, control_mid, control_coarse)
    ]
    members = members.reshape(held * members.shape[2], members.shape[3])
    controls = [c.reshape(held * c.shape[2], c.shape[3]) for c in (control_fine, control_mid, control_coarse)]
    in_hbm = [pltpu.with_memory_space_constraint(c, pltpu.HBM) for c in controls]
    sizes = tuple(c.shape for c in controls)
    all_cells = sum(cells for cells, _ in sizes)
    fine_cells, fine_rows = sizes[0]
    out_cells = fine_cells // 2
    tiles = 4 * held
    span = held * REACH

    edge, odd_main, even_main = call(
        edge_kernel,
        [((REACH, all_cells), B16)] + [((tiles, REACH, 128), B16)] * 2,
        [HBM] * 3,
        [pltpu.VMEM((cells // span, held, REACH, min(rows, 128)), B16) for cells, rows in sizes]
        + [pltpu.VMEM((held, REACH, sizes[2][1]), B16), pltpu.SemaphoreType.DMA((14,))],
        flops=10**7,
    )(*raw)
    count = lax.axis_size("lon")
    odd_pairs = [(i, (i + 1) % count) for i in range(1, count, 2)]
    odd_pairs += [(j, i) for i, j in odd_pairs]
    even_pairs = [(i, i + 1) for i in range(0, count, 2)]
    even_pairs += [(j, i) for i, j in even_pairs]
    arrived = lax.ppermute(edge, "lat", [(0, 1), (1, 0)])
    odd = lax.ppermute(odd_main, "lon", odd_pairs)

    outs = [((cells, fine_rows), F32) for cells, _ in sizes]
    outs += [((rows, fine_rows), B16) for _, rows in sizes]
    outs += [((3, REACH, fine_rows), B16)]
    outs += [((out_cells, cells // 2), B16) for cells, _ in sizes]
    outs += [((LEV * factor * REACH, 2 * LEV * REACH), B16) for factor in FACTORS]
    outs += [((fine_cells, fine_rows), B16)] * 2
    prep = call(
        functools.partial(prep_kernel, sizes),
        outs,
        [SMEM] + [VMEM] * 4 + [HBM] * 3,
        [pltpu.VMEM((256, 256), B16)] + [pltpu.VMEM(s, B16) for s in sizes] + [pltpu.SemaphoreType.DMA((3,))],
        flops=10**9,
    )(band_radii, members, vertical, mid_picks[None], coarse_picks[None], *in_hbm)
    xr, rows, rim, own, side, res = prep[0:3], prep[3:6], prep[6], prep[7:10], prep[10:13], prep[13:15]

    odd_rim, even = call(
        functools.partial(forward_kernel, sizes),
        [((REACH, 3 * span), B16), ((tiles + 3 * span // 128, REACH, 128), B16)],
        [VMEM] * 2,
        flops=10**6,
    )(arrived, even_main)
    odd_rim = lax.ppermute(odd_rim, "lon", odd_pairs)
    even = lax.ppermute(even, "lon", even_pairs)

    partial = call(
        functools.partial(own_kernel, sizes), [((out_cells, fine_rows), F32)], [VMEM] * 11, flops=10**9
    )(arrived, *xr, rim, *own, members, *res)
    field = call(
        functools.partial(side_kernel, sizes),
        [((out_cells, fine_rows), B16)],
        [VMEM] * 15,
        [pltpu.VMEM((LEV, out_cells // LEV, fine_rows), F32)],
        flops=10**9,
    )(
        odd.reshape(tiles * REACH, 128),
        odd_rim,
        even.reshape(-1, 128),
        even,
        *rows,
        rim,
        *side,
        members,
        *res,
        partial,
    )

    blocks = field.reshape(devices, out_cells // devices, fine_rows)
    blocks = lax.all_to_all(blocks, "mem", split_axis=0, concat_axis=0, tiled=True)
    increment = blocks.astype(F32).sum(axis=0) / math.sqrt(member_total - 1)
    return increment[None, :, :]


def solution(mesh):
    placed = (
        P("mem", None, "lon", "lat"),
        P("mem", None, "lon", "lat"),
        P("mem", None, "lon", "lat"),
        P("mem", None, "lon", "lat"),
        P(),
        P(),
        P(),
        P(),
    )
    return jax.shard_map(on_device, mesh=mesh, in_specs=placed, out_specs=P("lon", "mem", "lat"), check_vma=False)
```

time: 63.5 us -> 68.3 us (1.076)
  starting transfers between devices: 12.9 us -> 17.6 us
  local copies, waits for them, and re-layouts: 1.69 us -> 0.67 us
  Pallas kernels: 7.39 us -> 8.22 us
    ppermute x2 -> x3, starting transfers between devices: 4.71 us -> 9.42 us  [the longest x1 5.57 us: on_device(): odd = lax.ppermute(odd_main, 'lon', odd_pairs)]
    ppermute x1, waiting for transfers between devices: 0.01 us -> 1.86 us  [on_device(): arrived = lax.ppermute(edge, 'lat', [(0, 1), (1, 0)])]
    ppermute x2 -> x3, waiting for transfers between devices: 4.86 us -> 3.24 us  [the longest x1 3.24 us: on_device(): odd_rim = lax.ppermute(odd_rim, 'lon', odd_pairs)]
    unnamed x16 -> x10, local copies, waits for them, and re-layouts: 1.69 us -> 0.66 us
    pallas_call x5, Pallas kernels: 7.39 us -> 8.22 us  [run(): return kernel_call(*args, **kwargs)(*operands)]
  transfers between devices with their start and end apart: 3 -> 4, of which waited for: 1 -> 2; matrix products, arithmetic and copies ran while one was open for 0% -> 0% of each run, Pallas kernels for 7% -> 8%
where the time goes in v3:
time: 68.3 us; the launch traced here: 67.9 us
  blocking collectives  35.5 us (52%)
  starting transfers between devices  17.6 us (26%)
  Pallas kernels  8.22 us (12%)
  waiting for transfers between devices  5.1 us (7%)
    all_to_all x1, blocking collectives, on_device(): lax.all_to_all(blocks, 'mem', split_axis=0, concat_axis=0, tiled=True)  35.5 us
    pallas_call x5, Pallas kernels, run(): return kernel_call(*args, **kwargs)(*operands)  8.22 us
    ppermute x1, starting transfers between devices, on_device(): arrived = lax.ppermute(edge, 'lat', [(0, 1), (1, 0)])  8.19 us
    ppermute x1, starting transfers between devices, on_device(): odd = lax.ppermute(odd_main, 'lon', odd_pairs)  5.57 us
    ppermute x1, waiting for transfers between devices, on_device(): odd_rim = lax.ppermute(odd_rim, 'lon', odd_pairs)  3.24 us
    ppermute x1, starting transfers between devices, on_device(): odd_rim = lax.ppermute(odd_rim, 'lon', odd_pairs)  1.92 us
    ppermute x1, starting transfers between devices, on_device(): even = lax.ppermute(even, 'lon', even_pairs)  1.92 us
    ppermute x1, waiting for transfers between devices, on_device(): arrived = lax.ppermute(edge, 'lat', [(0, 1), (1, 0)])  1.86 us
  transfers between devices with their start and end apart: 4, of which 2 were waited for; matrix products, arithmetic and copies ran while one was open for 0% of the time, Pallas kernels for 8%

profile of v3, /device:TPU:2, one launch (start us, length us, event | category | flops | bytes accessed | tf_op | source)
XLA Modules:
  0.0 67.9 jit_solution(17568943842258132983)
XLA Ops:
  0.0 0.0 copy-start
  0.0 1.5 %shard_map.82 = (bf16[8,1792]{1,0:T(8,128)(2,1)S(1)}, bf16[128,8,128]{2,1,0:T(8,128)(2,1)S(1)}, bf16[128,8,128]{2,1,0:T(8,128)(2,1)S(1)}) custom-call(bf16[32,32,256]{2,1,0:T(8,128)(2,1)} %bitcast.20, bf16[32,16,128]{2,1,0:T(8,128)(2,1)} %bitcast.22, bf16[32,8,64]{2,1,0:T(8,128)(2,1)} %bitcast.24), custom_call_target="tpu_custom_call" | custom-call | flops 10000000 | bytes 1048576 | tf_op jit(solution)/shard_map/pallas_call | solution.py:294
  1.5 8.2 %collective-permute-start.1 = (bf16[8,1792]{1,0:T(8,128)(2,1)S(1)}, bf16[8,1792]{1,0:T(8,128)(2,1)S(1)}, u32[]{:S(2)}, u32[]{:S(2)}) collective-permute-start(bf16[8,1792]{1,0:T(8,128)(2,1)S(1)} %get-tuple-element.26), channel_id=1, source_target_pairs={{0,8},{8,0},{1,9},{9,1},{2,10},{10,2},{3,11},{11,3},{4,12},{12,4},... | collective-permute-start | bytes 86024 | tf_op jit(solution)/shard_map/ppermute | solution.py:353
  9.7 1.9 %collective-permute-done.1.rim_in = bf16[8,1792]{1,0:T(8,128)(2,1)S(1)} collective-permute-done((bf16[8,1792]{1,0:T(8,128)(2,1)S(1)}, bf16[8,1792]{1,0:T(8,128)(2,1)S(1)}, u32[]{:S(2)}, u32[]{:S(2)}) %collective-permute-start.1) | collective-permute-done | bytes 28704 | tf_op jit(solution)/shard_map/ppermute | solution.py:353
  11.6 0.0 copy-start.4
  11.6 0.0 copy-start.1
  11.6 1.9 %collective-permute-start.3 = (bf16[134,8,128]{2,1,0:T(8,128)(2,1)S(1)}, bf16[134,8,128]{2,1,0:T(8,128)(2,1)S(1)}, u32[]{:S(2)}, u32[]{:S(2)}) collective-permute-start(bf16[134,8,128]{2,1,0:T(8,128)(2,1)S(1)} %get-tuple-element.29), channel_id=1, source_target_pairs={{0,1},{2,3},{4,5},{6,7},{1,0},{3,2},{5,4},{7,6},{8,9},{10,11},{12,... | collective-permute-start | bytes 823304 | tf_op jit(solution)/shard_map/ppermute | solution.py:378
  13.5 5.6 %collective-permute-start = (bf16[128,8,128]{2,1,0:T(8,128)(2,1)S(1)}, bf16[128,8,128]{2,1,0:T(8,128)(2,1)S(1)}, u32[]{:S(2)}, u32[]{:S(2)}) collective-permute-start(bf16[128,8,128]{2,1,0:T(8,128)(2,1)S(1)} %get-tuple-element.25), channel_id=1, source_target_pairs={{1,2},{3,4},{5,6},{7,0},{2,1},{4,3},{6,5},{0,7},{9,10},{11,12},{13... | collective-permute-start | bytes 786440 | tf_op jit(solution)/shard_map/ppermute | solution.py:354
  19.1 0.0 copy-done.4
  19.1 0.0 copy-start.2
  19.1 0.0 copy-start.3
  19.2 0.0 copy-done
  19.2 0.0 copy-done.1
  19.2 0.6 copy-done.2
  19.8 0.0 copy-done.3
  19.8 4.0 %shard_map.84 = (f32[1024,256]{1,0:T(8,128)S(1)}, f32[512,256]{1,0:T(8,128)S(1)}, f32[256,256]{1,0:T(8,128)S(1)}, bf16[256,256]{1,0:T(8,128)(2,1)S(1)}, bf16[128...) custom-call(s32[3]{0:T(128)S(1)} %copy-done.3, ...), custom_call_target="tpu_custom_call" | custom-call | flops 1000000000 | bytes 1048576 | tf_op jit(solution)/shard_map/pallas_call | solution.py:294
  23.8 1.9 %collective-permute-start.2 = (bf16[8,768]{1,0:T(8,128)(2,1)S(1)}, bf16[8,768]{1,0:T(8,128)(2,1)S(1)}, u32[]{:S(2)}, u32[]{:S(2)}) collective-permute-start(bf16[8,768]{1,0:T(8,128)(2,1)S(1)} %get-tuple-element.28), channel_id=1, source_target_pairs={{1,2},{3,4},{5,6},{7,0},{2,1},{4,3},{6,5},{0,7},{9,10},{11,12},{13... | collective-permute-start | bytes 36872 | tf_op jit(solution)/shard_map/ppermute | solution.py:377
  25.7 1.6 %shard_map.85.partial = f32[512,256]{1,0:T(8,128)S(1)} custom-call(bf16[8,1792]{1,0:T(8,128)(2,1)S(1)} %collective-permute-done.1.rim_in, f32[1024,256]{1,0:T(8,128)S(1)} %get-tuple-element.39.xr0, f32[512,256]{1,0:T(8,128)S(1)} %get-tuple-element.40.xr1, f32[256,256]{1,0:T(8,128)S(1)} %get-tuple-element.41.xr2, ...), custom_call_target="tpu_custom_call" | custom-call | flops 1000000000 | bytes 1048576 | tf_op jit(solution)/shard_map/pallas_call | solution.py:294
  27.4 3.2 %collective-permute-done.2.odd_rim = bf16[8,768]{1,0:T(8,128)(2,1)S(1)} collective-permute-done((bf16[8,768]{1,0:T(8,128)(2,1)S(1)}, bf16[8,768]{1,0:T(8,128)(2,1)S(1)}, u32[]{:S(2)}, u32[]{:S(2)}) %collective-permute-start.2) | collective-permute-done | bytes 12320 | tf_op jit(solution)/shard_map/ppermute | solution.py:377
  30.6 0.0 collective-permute-done
  30.6 0.0 collective-permute-done.3.even_rim
  30.6 1.1 %shard_map.86 = bf16[512,256]{1,0:T(8,128)(2,1)S(1)} custom-call(bf16[1024,128]{1,0:T(8,128)(2,1)S(1)} %bitcast.18, bf16[8,768]{1,0:T(8,128)(2,1)S(1)} %collective-permute-done.2.odd_rim, bf16[1072,128]{1,0:T(8,128)(2,1)S(1)} %bitcast.16, bf16[134,8,128]{2,1,0:T(8,128)(2,1)S(1)} %collective-permute-done.3.even_rim, ...), custom_call_target="tpu_custom_call" | custom-call | flops 1000000000 | bytes 1048576 | tf_op jit(solution)/shard_map/pallas_call | solution.py:294
  31.7 35.5 %all_to_all.5 = bf16[64,8,256]{2,1,0:T(8,128)(2,1)S(1)} all-to-all(bf16[64,8,256]{2,1,0:T(8,128)(2,1)S(1)} %bitcast.17), channel_id=1, replica_groups=mesh['mem'=64,'lat'=2,'lon'=8] {'mem'}, dimensions={0} | all-to-all | bytes 524288 | tf_op jit(solution)/shard_map/all_to_all | solution.py:403
  67.2 0.1 convert_reduce_fusion
  67.3 0.6 multiply_bitcast_fusion
  (2 shorter events, 0.0 us)
Async XLA Ops:
  0.0 19.2 %copy-start = (bf16[2,16,32,256]{3,2,1,0:T(8,128)(2,1)S(1)}, bf16[2,16,32,256]{3,2,1,0:T(8,128)(2,1)}, u32[]{:S(2)}) copy-start(bf16[2,16,32,256]{3,2,1,0:T(8,128)(2,1)} %param.8) | copy-start | bytes 1572868
  1.5 10.1 %collective-permute-start.1 = (bf16[8,1792]{1,0:T(8,128)(2,1)S(1)}, bf16[8,1792]{1,0:T(8,128)(2,1)S(1)}, u32[]{:S(2)}, u32[]{:S(2)}) collective-permute-start(bf16[8,1792]{1,0:T(8,128)(2,1)S(1)} %get-tuple-element.26), channel_id=1, source_target_pairs={{0,8},{8,0},{1,9},{9,1},{2,10},{10,2},{3,11},{11,3},{4,12},{12,4},... | collective-permute-start | bytes 86024 | tf_op jit(solution)/shard_map/ppermute | solution.py:353
  11.6 7.6 %copy-start.4 = (s32[384]{0:T(512)S(1)}, s32[384]{0:T(512)}, u32[]{:S(2)}) copy-start(s32[384]{0:T(512)} %param.13) | copy-start | bytes 4612
  11.6 7.6 %copy-start.1 = (bf16[3,16,16]{2,1,0:T(8,128)(2,1)S(1)}, bf16[3,16,16]{2,1,0:T(8,128)(2,1)}, u32[]{:S(2)}) copy-start(bf16[3,16,16]{2,1,0:T(8,128)(2,1)} %vertical.1) | copy-start | bytes 4612
  11.6 19.0 %collective-permute-start.3 = (bf16[134,8,128]{2,1,0:T(8,128)(2,1)S(1)}, bf16[134,8,128]{2,1,0:T(8,128)(2,1)S(1)}, u32[]{:S(2)}, u32[]{:S(2)}) collective-permute-start(bf16[134,8,128]{2,1,0:T(8,128)(2,1)S(1)} %get-tuple-element.29), channel_id=1, source_target_pairs={{0,1},{2,3},{4,5},{6,7},{1,0},{3,2},{5,4},{7,6},{8,9},{10,11},{12,... | collective-permute-start | bytes 823304 | tf_op jit(solution)/shard_map/ppermute | solution.py:378
  13.5 17.1 %collective-permute-start = (bf16[128,8,128]{2,1,0:T(8,128)(2,1)S(1)}, bf16[128,8,128]{2,1,0:T(8,128)(2,1)S(1)}, u32[]{:S(2)}, u32[]{:S(2)}) collective-permute-start(bf16[128,8,128]{2,1,0:T(8,128)(2,1)S(1)} %get-tuple-element.25), channel_id=1, source_target_pairs={{1,2},{3,4},{5,6},{7,0},{2,1},{4,3},{6,5},{0,7},{9,10},{11,12},{13... | collective-permute-start | bytes 786440 | tf_op jit(solution)/shard_map/ppermute | solution.py:354
  19.1 0.7 %copy-start.2 = (s32[192]{0:T(256)S(1)}, s32[192]{0:T(256)}, u32[]{:S(2)}) copy-start(s32[192]{0:T(256)} %param.14) | copy-start | bytes 2308
  19.1 0.7 copy-start.3
  23.8 6.8 %collective-permute-start.2 = (bf16[8,768]{1,0:T(8,128)(2,1)S(1)}, bf16[8,768]{1,0:T(8,128)(2,1)S(1)}, u32[]{:S(2)}, u32[]{:S(2)}) collective-permute-start(bf16[8,768]{1,0:T(8,128)(2,1)S(1)} %get-tuple-element.28), channel_id=1, source_target_pairs={{1,2},{3,4},{5,6},{7,0},{2,1},{4,3},{6,5},{0,7},{9,10},{11,12},{13... | collective-permute-start | bytes 36872 | tf_op jit(solution)/shard_map/ppermute | solution.py:377

commit v4 on v3

--- a/solution.py
+++ b/solution.py
@@ -24,21 +24,24 @@
     return lax.dot_general(a, b, (((ca,), (cb,)), ((), ())), preferred_element_type=F32)
 
 
-def bell(offset, radius):
-    wide = offset.astype(F32)
+def tap_table(radius):
+    lane = iota((8, 128), 1)
+    wide = (lane - REACH).astype(F32)
     reach_now = jnp.broadcast_to(radius.astype(F32), wide.shape)
     raw = jnp.exp(-0.5 * jnp.square(wide / (0.5 * reach_now)))
-    return jnp.where(jnp.abs(wide) <= reach_now, raw, 0.0)
-
-
-def bell_sum(radius):
-    lanes = iota((8, 128), 1)
-    raw = jnp.where(lanes <= 2 * REACH, bell(lanes - REACH, radius), 0.0)
-    return jnp.sum(raw, axis=1, keepdims=True)[0:1]
-
-
-def taps(offset, radius, total):
-    return (bell(offset, radius) / total).astype(B16)
+    raw = jnp.where((jnp.abs(wide) <= reach_now) & (lane <= 2 * REACH), raw, 0.0)
+    weights = raw / jnp.sum(raw, axis=1, keepdims=True)
+    return weights.astype(B16).astype(F32)[0:1]
+
+
+def taps(offset, table):
+    lane = jnp.where(jnp.abs(offset) <= REACH, offset + REACH, 127)
+    full = jnp.broadcast_to(table, (offset.shape[0], 128))
+    parts = [
+        jnp.take_along_axis(full, lane[:, at : at + 128], axis=1, mode="promise_in_bounds")
+        for at in range(0, offset.shape[1], 128)
+    ]
+    return parts[0] if len(parts) == 1 else jnp.concatenate(parts, axis=1)
 
 
 def edge_kernel(fine, mid, coarse, out, odd, even, buf0, buf1, buf2, buf3, sems):
@@ -92,12 +95,6 @@
     vertical,
     mid_picks,
     coarse_picks,
-    fine,
-    mid,
-    coarse,
-    xr0,
-    xr1,
-    xr2,
     row0,
     row1,
     row2,
@@ -111,28 +108,19 @@
     res1,
     res2,
     spare,
-    buf0,
-    buf1,
-    buf2,
-    sems,
 ):
     lat = lax.axis_index("lat")
     lon = lax.axis_index("lon")
     cols = 32
-    copies = []
-    for band, (ref, buf) in enumerate(zip((fine, mid, coarse), (buf0, buf1, buf2))):
-        copies.append(pltpu.make_async_copy(ref, buf, sems.at[band]))
-        copies[band].start()
     refs = zip((row0, row1, row2), (own0, own1, own2), (side0, side1, side2))
     for band, (factor, (cells, rows), (row_ref, own_ref, side_ref)) in enumerate(zip(FACTORS, sizes, refs)):
-        radius = radii[band]
-        total = bell_sum(radius)
+        table = tap_table(radii[band])
         width = cols // factor
         shape = (rows, rows * factor)
-        row_ref[...] = taps(iota(shape, 0) - iota(shape, 1) // factor, radius, total)
+        row_ref[...] = taps(iota(shape, 0) - iota(shape, 1) // factor, table).astype(B16)
         base = jnp.where(lat == 0, rows, -REACH)
         shape = (REACH, rows * factor)
-        rim[band] = taps(iota(shape, 0) + base - iota(shape, 1) // factor, radius, total)
+        rim[band] = taps(iota(shape, 0) + base - iota(shape, 1) // factor, table).astype(B16)
         reach_cols = factor * REACH
         parts = (
             (own_ref, 0, width, cols, 0, 0),
@@ -143,34 +131,37 @@
             lanes = LEV * span
             place = iota((count, lanes), 1) % span + shift
             target = (iota((count, lanes), 0) + first) // factor
-            pattern = taps(place - target, radius, total).astype(F32)
+            pattern = taps(place - target, table)
             level = (iota((LEV, lanes), 0) == iota((LEV, lanes), 1) // span).astype(B16)
             spread = dot(vertical[band], level)
             for k in range(LEV):
                 to[k * count : (k + 1) * count, at : at + lanes] = (spread[k : k + 1] * pattern).astype(B16)
-    for copy, buf, row_ref, xr in zip(copies, (buf0, buf1, buf2), (row0, row1, row2), (xr0, xr1, xr2)):
-        copy.wait()
-        xr[...] = dot(buf[...], row_ref[...])
     full_rows = sizes[0][1]
     block = 8 * cols
     for factor, picks, out in ((2, mid_picks, res1), (4, coarse_picks, res2)):
-        n = picks.shape[1]
         rows = full_rows // factor
         width = cols // factor
-        values = jnp.broadcast_to(picks[...].astype(F32), (8, n)).astype(B16)
-        shape = (n, full_rows)
-        hot = (iota(shape, 0) == lat * rows + iota(shape, 1) // factor).astype(B16)
-        chosen = dot(values, hot)[0:1]
-        shape = (full_rows, full_rows)
-        wanted = (factor * (iota((1, full_rows), 1) // factor)).astype(F32) + chosen
-        row_pick = (iota(shape, 0).astype(F32) == wanted).astype(B16)
-        shape = (cols, n)
-        hot = (iota(shape, 1) == 2 * rows + lon * width + iota(shape, 0) // factor).astype(B16)
-        chosen = dot(hot, values, 1, 1)[:, 0:1]
-        wanted = (factor * (iota((cols, 1), 0) // factor)).astype(F32) + chosen
-        lanes = iota((cols, block), 1).astype(F32)
+        total = 2 * rows
+        values = jnp.broadcast_to(picks[...].astype(F32), (8, picks.shape[1])).astype(B16)
+        if rows == 128:
+            along = jnp.where(lat == 0, values[:, :128].astype(F32), values[:, 128:256].astype(F32)).astype(B16)
+            start = 0
+        else:
+            along = values[:, :128]
+            start = lat * rows
+        shape = (128, full_rows)
+        hot = (iota(shape, 0) == start + iota(shape, 1) // factor).astype(B16)
+        chosen = dot(along, hot)[0:1].astype(jnp.int32)
+        wanted = factor * (iota((1, full_rows), 1) // factor) + chosen
+        row_pick = (iota((full_rows, full_rows), 0) == wanted).astype(B16)
+        across = values[:, total:]
+        shape = (cols, across.shape[1])
+        hot = (iota(shape, 1) == lon * width + iota(shape, 0) // factor).astype(B16)
+        chosen = dot(hot, across, 1, 1)[:, 0:1].astype(jnp.int32)
+        wanted = factor * (iota((cols, 1), 0) // factor) + chosen
+        lanes = iota((cols, block), 1)
         for k in range(8):
-            spare[k * cols : (k + 1) * cols] = (lanes == wanted + F32(k * cols)).astype(B16)
+            spare[k * cols : (k + 1) * cols] = (lanes == wanted + k * cols).astype(B16)
         col_pick = spare[...]
         for part in range(members.shape[0] // block):
             at = slice(part * block, (part + 1) * block)
@@ -193,18 +184,20 @@
         start += cells
 
 
-def own_kernel(sizes, rim_in, xr0, xr1, xr2, rim, own0, own1, own2, members, res1, res2, out):
+def own_kernel(
+    sizes, rim_in, fine, mid, coarse, row0, row1, row2, rim, own0, own1, own2, members, res1, res2, out
+):
     first = True
     start = 0
     held = 2 * LEV
-    bands = zip(FACTORS, sizes, (xr0, xr1, xr2), (own0, own1, own2), (members, res1, res2))
-    for band, (factor, (cells, rows), xr, own, res) in enumerate(bands):
+    refs = zip((fine, mid, coarse), (row0, row1, row2), (own0, own1, own2), (members, res1, res2))
+    for band, (factor, (cells, rows), (ref, row_ref, own, res)) in enumerate(zip(FACTORS, sizes, refs)):
         width = cells // held
         size = res.shape[0] // 2
         edge = rim[band]
         span = LEV * REACH
         for m in range(2):
-            sums = xr[m * cells // 2 : (m + 1) * cells // 2].reshape(LEV, width, -1)
+            sums = dot(ref[m * cells // 2 : (m + 1) * cells // 2], row_ref[...]).reshape(LEV, width, -1)
             parts = []
             for group in range(width // REACH):
                 at = start + (2 * group + m) * span
@@ -329,7 +322,6 @@
     ]
     members = members.reshape(held * members.shape[2], members.shape[3])
     controls = [c.reshape(held * c.shape[2], c.shape[3]) for c in (control_fine, control_mid, control_coarse)]
-    in_hbm = [pltpu.with_memory_space_constraint(c, pltpu.HBM) for c in controls]
     sizes = tuple(c.shape for c in controls)
     all_cells = sum(cells for cells, _ in sizes)
     fine_cells, fine_rows = sizes[0]
@@ -353,20 +345,15 @@
     arrived = lax.ppermute(edge, "lat", [(0, 1), (1, 0)])
     odd = lax.ppermute(odd_main, "lon", odd_pairs)
 
-    outs = [((cells, fine_rows), F32) for cells, _ in sizes]
-    outs += [((rows, fine_rows), B16) for _, rows in sizes]
+    outs = [((rows, fine_rows), B16) for _, rows in sizes]
     outs += [((3, REACH, fine_rows), B16)]
     outs += [((out_cells, cells // 2), B16) for cells, _ in sizes]
     outs += [((LEV * factor * REACH, 2 * LEV * REACH), B16) for factor in FACTORS]
     outs += [((fine_cells, fine_rows), B16)] * 2
     prep = call(
-        functools.partial(prep_kernel, sizes),
-        outs,
-        [SMEM] + [VMEM] * 4 + [HBM] * 3,
-        [pltpu.VMEM((256, 256), B16)] + [pltpu.VMEM(s, B16) for s in sizes] + [pltpu.SemaphoreType.DMA((3,))],
-        flops=10**9,
-    )(band_radii, members, vertical, mid_picks[None], coarse_picks[None], *in_hbm)
-    xr, rows, rim, own, side, res = prep[0:3], prep[3:6], prep[6], prep[7:10], prep[10:13], prep[13:15]
+        functools.partial(prep_kernel, sizes), outs, [SMEM] + [VMEM] * 4, [pltpu.VMEM((256, 256), B16)], flops=10**9
+    )(band_radii, members, vertical, mid_picks[None], coarse_picks[None])
+    rows, rim, own, side, res = prep[0:3], prep[3], prep[4:7], prep[7:10], prep[10:12]
 
     odd_rim, even = call(
         functools.partial(forward_kernel, sizes),
@@ -378,8 +365,8 @@
     even = lax.ppermute(even, "lon", even_pairs)
 
     partial = call(
-        functools.partial(own_kernel, sizes), [((out_cells, fine_rows), F32)], [VMEM] * 11, flops=10**9
-    )(arrived, *xr, rim, *own, members, *res)
+        functools.partial(own_kernel, sizes), [((out_cells, fine_rows), F32)], [VMEM] * 14, flops=10**9
+    )(arrived, *controls, *rows, rim, *own, members, *res)
     field = call(
         functools.partial(side_kernel, sizes),
         [((out_cells, fine_rows), B16)],

time: 68.3 us -> 66.1 us (0.968)
  the two profiles are of different devices: /device:TPU:2 before, /device:TPU:113 now
where the time goes in v4:
time: 66.1 us; the launch traced here: 65.7 us
  blocking collectives  30.2 us (46%)
  starting transfers between devices  20.1 us (30%)
  waiting for transfers between devices  7.55 us (11%)
  Pallas kernels  6.34 us (10%)
  local copies, waits for them, and re-layouts  0.68 us (1%)
  other arithmetic  0.67 us (1%)
    all_to_all x1, blocking collectives, on_device(): lax.all_to_all(blocks, 'mem', split_axis=0, concat_axis=0, tiled=True)  30.2 us
    ppermute x1, starting transfers between devices, on_device(): odd = lax.ppermute(odd_main, 'lon', odd_pairs)  10.5 us
    pallas_call x5, Pallas kernels, run(): return kernel_call(*args, **kwargs)(*operands)  6.34 us
    ppermute x1, waiting for transfers between devices, on_device(): arrived = lax.ppermute(edge, 'lat', [(0, 1), (1, 0)])  4.55 us
    ppermute x1, starting transfers between devices, on_device(): arrived = lax.ppermute(edge, 'lat', [(0, 1), (1, 0)])  3.98 us
    ppermute x1, starting transfers between devices, on_device(): even = lax.ppermute(even, 'lon', even_pairs)  3.73 us
    ppermute x1, waiting for transfers between devices, on_device(): odd_rim = lax.ppermute(odd_rim, 'lon', odd_pairs)  3 us
    ppermute x1, starting transfers between devices, on_device(): odd_rim = lax.ppermute(odd_rim, 'lon', odd_pairs)  1.92 us
  transfers between devices with their start and end apart: 4, of which 2 were waited for; matrix products, arithmetic and copies ran while one was open for 0% of the time, Pallas kernels for 6%

profile of v4, /device:TPU:113, one launch (start us, length us, event | category | flops | bytes accessed | tf_op | source)
XLA Modules:
  0.0 65.7 jit_solution(17944493247986385167)
XLA Ops:
  0.0 0.0 copy-start.1
  0.0 1.5 %shard_map.82 = (bf16[8,1792]{1,0:T(8,128)(2,1)S(1)}, bf16[128,8,128]{2,1,0:T(8,128)(2,1)S(1)}, bf16[128,8,128]{2,1,0:T(8,128)(2,1)S(1)}) custom-call(bf16[32,32,256]{2,1,0:T(8,128)(2,1)} %bitcast.13, bf16[32,16,128]{2,1,0:T(8,128)(2,1)} %bitcast.20, bf16[32,8,64]{2,1,0:T(8,128)(2,1)} %bitcast.22), custom_call_target="tpu_custom_call" | custom-call | flops 10000000 | bytes 1048576 | tf_op jit(solution)/shard_map/pallas_call | solution.py:287
  1.5 4.0 %collective-permute-start.1 = (bf16[8,1792]{1,0:T(8,128)(2,1)S(1)}, bf16[8,1792]{1,0:T(8,128)(2,1)S(1)}, u32[]{:S(2)}, u32[]{:S(2)}) collective-permute-start(bf16[8,1792]{1,0:T(8,128)(2,1)S(1)} %get-tuple-element.23), channel_id=1, source_target_pairs={{0,8},{8,0},{1,9},{9,1},{2,10},{10,2},{3,11},{11,3},{4,12},{12,4},... | collective-permute-start | bytes 86024 | tf_op jit(solution)/shard_map/ppermute | solution.py:345
  5.5 4.5 %collective-permute-done.1.rim_in = bf16[8,1792]{1,0:T(8,128)(2,1)S(1)} collective-permute-done((bf16[8,1792]{1,0:T(8,128)(2,1)S(1)}, bf16[8,1792]{1,0:T(8,128)(2,1)S(1)}, u32[]{:S(2)}, u32[]{:S(2)}) %collective-permute-start.1) | collective-permute-done | bytes 28704 | tf_op jit(solution)/shard_map/ppermute | solution.py:345
  10.0 0.0 copy-start.4
  10.1 0.0 copy-start.7
  10.1 3.7 %collective-permute-start.3 = (bf16[134,8,128]{2,1,0:T(8,128)(2,1)S(1)}, bf16[134,8,128]{2,1,0:T(8,128)(2,1)S(1)}, u32[]{:S(2)}, u32[]{:S(2)}) collective-permute-start(bf16[134,8,128]{2,1,0:T(8,128)(2,1)S(1)} %get-tuple-element.26), channel_id=1, source_target_pairs={{0,1},{2,3},{4,5},{6,7},{1,0},{3,2},{5,4},{7,6},{8,9},{10,11},{12,... | collective-permute-start | bytes 823304 | tf_op jit(solution)/shard_map/ppermute | solution.py:365
  13.8 10.5 %collective-permute-start = (bf16[128,8,128]{2,1,0:T(8,128)(2,1)S(1)}, bf16[128,8,128]{2,1,0:T(8,128)(2,1)S(1)}, u32[]{:S(2)}, u32[]{:S(2)}) collective-permute-start(bf16[128,8,128]{2,1,0:T(8,128)(2,1)S(1)} %get-tuple-element.22), channel_id=1, source_target_pairs={{1,2},{3,4},{5,6},{7,0},{2,1},{4,3},{6,5},{0,7},{9,10},{11,12},{13... | collective-permute-start | bytes 786440 | tf_op jit(solution)/shard_map/ppermute | solution.py:346
  24.3 0.0 copy-done.7
  24.3 0.0 copy-start.5
  24.3 0.0 copy-start.6
  24.3 0.0 copy-done.1
  24.3 0.0 copy-done.4
  24.3 0.6 copy-done.5
  25.0 0.0 copy-done.6
  25.0 0.0 copy-start
  25.0 0.0 copy-start.2
  25.0 0.0 copy-start.3
  25.0 1.9 %shard_map.84 = (bf16[256,256]{1,0:T(8,128)(2,1)S(1)}, bf16[128,256]{1,0:T(8,128)(2,1)S(1)}, bf16[64,256]{1,0:T(8,128)(2,1)S(1)}, bf16[3,8,256]{2,1,0:T(8,128)(2...) custom-call(s32[3]{0:T(128)S(1)} %copy-done.6, ...), custom_call_target="tpu_custom_call" | custom-call | flops 1000000000 | bytes 1048576 | tf_op jit(solution)/shard_map/pallas_call | solution.py:287
  26.9 1.9 %collective-permute-start.2 = (bf16[8,768]{1,0:T(8,128)(2,1)S(1)}, bf16[8,768]{1,0:T(8,128)(2,1)S(1)}, u32[]{:S(2)}, u32[]{:S(2)}) collective-permute-start(bf16[8,768]{1,0:T(8,128)(2,1)S(1)} %get-tuple-element.25), channel_id=1, source_target_pairs={{1,2},{3,4},{5,6},{7,0},{2,1},{4,3},{6,5},{0,7},{9,10},{11,12},{13... | collective-permute-start | bytes 36872 | tf_op jit(solution)/shard_map/ppermute | solution.py:364
  28.8 0.0 copy-done
  28.8 0.0 copy-done.2
  28.8 0.0 copy-done.3
  28.8 1.8 %shard_map.85.partial = f32[512,256]{1,0:T(8,128)S(1)} custom-call(bf16[8,1792]{1,0:T(8,128)(2,1)S(1)} %collective-permute-done.1.rim_in, bf16[1024,256]{1,0:T(8,128)(2,1)S(1)} %bitcast.14, bf16[512,128]{1,0:T(8,128)(2,1)S(1)} %bitcast.21, bf16[256,64]{1,0:T(8,128)(2,1)S(1)} %bitcast.23, bf16[256,256]{1,0:T(8,128)(2,1)S(1)} %get-tuple-element.27.row0, ...), custom_call_target="tpu_custom_call" | custom-call | flops 1000000000 | bytes 1048576 | tf_op jit(solution)/shard_map/pallas_call | solution.py:287
  30.7 3.0 %collective-permute-done.2.odd_rim = bf16[8,768]{1,0:T(8,128)(2,1)S(1)} collective-permute-done((bf16[8,768]{1,0:T(8,128)(2,1)S(1)}, bf16[8,768]{1,0:T(8,128)(2,1)S(1)}, u32[]{:S(2)}, u32[]{:S(2)}) %collective-permute-start.2) | collective-permute-done | bytes 12320 | tf_op jit(solution)/shard_map/ppermute | solution.py:364
  33.7 0.0 collective-permute-done
  33.7 0.0 collective-permute-done.3.even_rim
  33.7 1.1 %shard_map.86 = bf16[512,256]{1,0:T(8,128)(2,1)S(1)} custom-call(bf16[1024,128]{1,0:T(8,128)(2,1)S(1)} %bitcast.24, bf16[8,768]{1,0:T(8,128)(2,1)S(1)} %collective-permute-done.2.odd_rim, bf16[1072,128]{1,0:T(8,128)(2,1)S(1)} %bitcast.18, bf16[134,8,128]{2,1,0:T(8,128)(2,1)S(1)} %collective-permute-done.3.even_rim, ...), custom_call_target="tpu_custom_call" | custom-call | flops 1000000000 | bytes 1048576 | tf_op jit(solution)/shard_map/pallas_call | solution.py:287
  34.8 30.2 %all_to_all.5 = bf16[64,8,256]{2,1,0:T(8,128)(2,1)S(1)} all-to-all(bf16[64,8,256]{2,1,0:T(8,128)(2,1)S(1)} %bitcast.19), channel_id=1, replica_groups=mesh['mem'=64,'lat'=2,'lon'=8] {'mem'}, dimensions={0} | all-to-all | bytes 524288 | tf_op jit(solution)/shard_map/all_to_all | solution.py:390
  65.0 0.1 convert_reduce_fusion
  65.1 0.6 multiply_bitcast_fusion
  (2 shorter events, 0.0 us)
Async XLA Ops:
  0.0 24.3 %copy-start.1 = (bf16[2,16,32,256]{3,2,1,0:T(8,128)(2,1)S(1)}, bf16[2,16,32,256]{3,2,1,0:T(8,128)(2,1)}, u32[]{:S(2)}) copy-start(bf16[2,16,32,256]{3,2,1,0:T(8,128)(2,1)} %param.8) | copy-start | bytes 1572868
  1.5 8.5 %collective-permute-start.1 = (bf16[8,1792]{1,0:T(8,128)(2,1)S(1)}, bf16[8,1792]{1,0:T(8,128)(2,1)S(1)}, u32[]{:S(2)}, u32[]{:S(2)}) collective-permute-start(bf16[8,1792]{1,0:T(8,128)(2,1)S(1)} %get-tuple-element.23), channel_id=1, source_target_pairs={{0,8},{8,0},{1,9},{9,1},{2,10},{10,2},{3,11},{11,3},{4,12},{12,4},... | collective-permute-start | bytes 86024 | tf_op jit(solution)/shard_map/ppermute | solution.py:345
  10.0 14.3 %copy-start.4 = (bf16[3,16,16]{2,1,0:T(8,128)(2,1)S(1)}, bf16[3,16,16]{2,1,0:T(8,128)(2,1)}, u32[]{:S(2)}) copy-start(bf16[3,16,16]{2,1,0:T(8,128)(2,1)} %vertical.1) | copy-start | bytes 4612
  10.1 14.2 %copy-start.7 = (s32[384]{0:T(512)S(1)}, s32[384]{0:T(512)}, u32[]{:S(2)}) copy-start(s32[384]{0:T(512)} %param.13) | copy-start | bytes 4612
  10.1 23.6 %collective-permute-start.3 = (bf16[134,8,128]{2,1,0:T(8,128)(2,1)S(1)}, bf16[134,8,128]{2,1,0:T(8,128)(2,1)S(1)}, u32[]{:S(2)}, u32[]{:S(2)}) collective-permute-start(bf16[134,8,128]{2,1,0:T(8,128)(2,1)S(1)} %get-tuple-element.26), channel_id=1, source_target_pairs={{0,1},{2,3},{4,5},{6,7},{1,0},{3,2},{5,4},{7,6},{8,9},{10,11},{12,... | collective-permute-start | bytes 823304 | tf_op jit(solution)/shard_map/ppermute | solution.py:365
  13.8 19.9 %collective-permute-start = (bf16[128,8,128]{2,1,0:T(8,128)(2,1)S(1)}, bf16[128,8,128]{2,1,0:T(8,128)(2,1)S(1)}, u32[]{:S(2)}, u32[]{:S(2)}) collective-permute-start(bf16[128,8,128]{2,1,0:T(8,128)(2,1)S(1)} %get-tuple-element.22), channel_id=1, source_target_pairs={{1,2},{3,4},{5,6},{7,0},{2,1},{4,3},{6,5},{0,7},{9,10},{11,12},{13... | collective-permute-start | bytes 786440 | tf_op jit(solution)/shard_map/ppermute | solution.py:346
  24.3 0.7 %copy-start.5 = (s32[192]{0:T(256)S(1)}, s32[192]{0:T(256)}, u32[]{:S(2)}) copy-start(s32[192]{0:T(256)} %param.14) | copy-start | bytes 2308
  24.3 0.7 %copy-start.6 = (s32[3]{0:T(128)S(1)}, s32[3]{0:T(128)}, u32[]{:S(2)}) copy-start(s32[3]{0:T(128)} %radii.1) | copy-start | bytes 40
  25.0 3.8 %copy-start = (bf16[2,16,32,256]{3,2,1,0:T(8,128)(2,1)S(1)}, bf16[2,16,32,256]{3,2,1,0:T(8,128)(2,1)}, u32[]{:S(2)}) copy-start(bf16[2,16,32,256]{3,2,1,0:T(8,128)(2,1)} %param.9) | copy-start | bytes 1572868
  25.0 3.8 %copy-start.2 = (bf16[2,16,16,128]{3,2,1,0:T(8,128)(2,1)S(1)}, bf16[2,16,16,128]{3,2,1,0:T(8,128)(2,1)}, u32[]{:S(2)}) copy-start(bf16[2,16,16,128]{3,2,1,0:T(8,128)(2,1)} %param.10) | copy-start | bytes 393220
  25.0 3.9 %copy-start.3 = (bf16[2,16,8,64]{3,2,1,0:T(8,128)(2,1)S(1)}, bf16[2,16,8,64]{3,2,1,0:T(8,128)(2,1)}, u32[]{:S(2)}) copy-start(bf16[2,16,8,64]{3,2,1,0:T(8,128)(2,1)} %param.11) | copy-start | bytes 98308
  26.9 6.8 %collective-permute-start.2 = (bf16[8,768]{1,0:T(8,128)(2,1)S(1)}, bf16[8,768]{1,0:T(8,128)(2,1)S(1)}, u32[]{:S(2)}, u32[]{:S(2)}) collective-permute-start(bf16[8,768]{1,0:T(8,128)(2,1)S(1)} %get-tuple-element.25), channel_id=1, source_target_pairs={{1,2},{3,4},{5,6},{7,0},{2,1},{4,3},{6,5},{0,7},{9,10},{11,12},{13... | collective-permute-start | bytes 36872 | tf_op jit(solution)/shard_map/ppermute | solution.py:364
